TPU v7x, 32 devices: a whole 2x2x4 slice. The times are simulated.
32 devices in a mesh: seq: 8 (over z, x), head: 4 (over y, core).
Axes of the slice: x: 2, y: 2, z: 4, core: 2. Of those that a mesh axis runs over, the one named last changes fastest.
Arguments:
- queries: bfloat16 [2048, 1024], P('seq', 'head'), may hold values from -6 to 6
- key_rows: bfloat16 [2048, 1024], P('seq', 'head'), may hold values from -6 to 6
- value_rows: bfloat16 [2048, 1024], P('seq', 'head'), may hold values from -6 to 6
- out_weight: bfloat16 [1024, 1024], P('head'), may hold values from -0.1875 to 0.1875
- cotangent: bfloat16 [2048, 1024], P('seq'), may hold values from -6 to 6
Outputs:
- mixed_out: bfloat16 [2048, 1024], P(('seq', 'head'))
- query_grad: bfloat16 [2048, 1024], P('seq', 'head')
- key_grad: bfloat16 [2048, 1024], P('seq', 'head')
- value_grad: bfloat16 [2048, 1024], P('seq', 'head')
All inputs are finite; a program needn't handle non-finite values.
Results may differ from a plain program's by a relative error of at most 0.023.
Values may be sent and summed in bfloat16 or wider, within the bound.
A program may use at most 64 MiB of HBM per device.

v0:
```python
import math

import jax
import jax.numpy as jnp
from jax import lax
from jax.sharding import PartitionSpec as P

HEAD_DIM = 64
BLOCK = 128
POOL_ROWS = 64


masked_score = -1000000000.0


def extended_2(cells, sides, width):
    for axis, dim in sides:
        count = lax.axis_size(axis)
        ends = count - 1
        head = lax.slice_in_dim(cells, 0, width, axis=dim)
        tail = lax.slice_in_dim(cells, cells.shape[dim] - width, cells.shape[dim], axis=dim)
        cells = jnp.concatenate(
            [
                lax.ppermute(tail, axis, [(i, (i + 1) % count) for i in range(ends)]),
                cells,
                lax.ppermute(head, axis, [((i + 1) % count, i) for i in range(ends)]),
            ],
            axis=dim,
        )
    return cells


def from_partner(block, axis, bit):
    count = lax.axis_size(axis)
    route = []
    for low in range(count):
        high = low | 1 << bit
        if high != low and high < count:
            route += [(low, high), (high, low)]
    return lax.ppermute(block, axis, route)


def attend(query_block, window_block, window_bias, coarse_rows):
    feature_width = query_block.shape[1]
    head_count = feature_width // HEAD_DIM
    blocks = query_block.shape[0] // BLOCK
    score_scale = 1.0 / math.sqrt(HEAD_DIM)
    query_tiles = query_block.astype(jnp.bfloat16).reshape(blocks, BLOCK, head_count, HEAD_DIM)
    window_tiles = window_block.astype(jnp.bfloat16).reshape(blocks + 2, BLOCK, 2 * feature_width)
    spread = jnp.concatenate([window_tiles[:-2], window_tiles[1:-1], window_tiles[2:]], axis=1)
    fine_keys = spread[:, :, :feature_width].reshape(blocks, 3 * BLOCK, head_count, HEAD_DIM)
    fine_values = spread[:, :, feature_width:].reshape(blocks, 3 * BLOCK, head_count, HEAD_DIM)
    bias_tiles = window_bias.reshape(blocks + 2, BLOCK)
    fine_bias = jnp.concatenate([bias_tiles[:-2], bias_tiles[1:-1], bias_tiles[2:]], axis=1)
    coarse_tiles = coarse_rows.astype(jnp.bfloat16)
    coarse_keys = coarse_tiles[:, :feature_width].reshape(-1, head_count, HEAD_DIM)
    coarse_values = coarse_tiles[:, feature_width:].reshape(-1, head_count, HEAD_DIM)
    fine_scores = (
        jnp.einsum("nqhd,nkhd->nhqk", query_tiles, fine_keys, preferred_element_type=jnp.float32)
        * score_scale
        + fine_bias[:, None, None, :]
    )
    coarse_scores = (
        jnp.einsum("nqhd,khd->nhqk", query_tiles, coarse_keys, preferred_element_type=jnp.float32)
        * score_scale
    )
    row_max = lax.stop_gradient(jnp.maximum(fine_scores.max(axis=-1), coarse_scores.max(axis=-1)))[
        ..., None
    ]
    fine_exp = jnp.exp(fine_scores - row_max)
    coarse_exp = jnp.exp(coarse_scores - row_max)
    denominator = fine_exp.sum(axis=-1, keepdims=True) + coarse_exp.sum(axis=-1, keepdims=True)
    fine_weights = (fine_exp / denominator).astype(jnp.bfloat16)
    coarse_weights = (coarse_exp / denominator).astype(jnp.bfloat16)
    mixed_heads = jnp.einsum(
        "nhqk,nkhd->nqhd", fine_weights, fine_values, preferred_element_type=jnp.float32
    )
    mixed_heads = mixed_heads + jnp.einsum(
        "nhqk,khd->nqhd", coarse_weights, coarse_values, preferred_element_type=jnp.float32
    )
    return mixed_heads.reshape(query_block.shape[0], feature_width).astype(jnp.bfloat16)


def local_attention(query_rows, window_rows, window_bias, coarse_rows):
    group_rows = math.gcd(query_rows.shape[0], 4 * BLOCK)
    group_total = query_rows.shape[0] // group_rows

    def one_group(group_index):
        return attend(query_rows, window_rows, window_bias, coarse_rows)

    pieces = lax.map(one_group, jnp.arange(group_total, dtype=jnp.int32))
    return pieces.reshape(query_rows.shape[0], query_rows.shape[1])


def pair_pool(panel):
    row_count = panel.shape[-2]
    paired = panel.reshape(panel.shape[:-2] + (row_count // 2, 2, panel.shape[-1]))
    return (paired[..., 0, :] + paired[..., 1, :]) / math.sqrt(2.0)


def pair_spread(panel_grad):
    return jnp.repeat(panel_grad, 2, axis=0) / math.sqrt(2.0)


def body(queries, key_rows, value_rows, out_weight, cotangent):
    frame_count = queries.shape[0]
    feature_width = queries.shape[1]
    seq_count = lax.axis_size("seq")
    position = lax.axis_index("seq")
    bit_total = seq_count.bit_length() - 1
    pool_span = frame_count // POOL_ROWS
    joined = jnp.concatenate([key_rows, value_rows], axis=1)
    extended = extended_2(joined, (("seq", 0),), BLOCK)
    positions = (
        position * frame_count - BLOCK + jnp.arange(frame_count + 2 * BLOCK, dtype=jnp.int32)
    )
    window_bias = jnp.where(
        (positions >= 0) & (positions < seq_count * frame_count), 0.0, masked_score
    ).astype(jnp.float32)
    own_panel = joined.reshape(POOL_ROWS, pool_span, 2 * feature_width).sum(
        axis=1, dtype=jnp.float32
    ) / math.sqrt(pool_span)
    partners = []
    current = own_panel
    for bit_index in range(bit_total):
        partner = from_partner(current, "seq", bit_index)
        partners.append(partner)
        upper_side = jnp.right_shift(position, bit_index) & 1 == 1
        lower_half = jnp.where(upper_side, partner, current)
        upper_half = jnp.where(upper_side, current, partner)
        current = jnp.concatenate([pair_pool(lower_half), pair_pool(upper_half)], axis=0)
    partner_rows = jnp.concatenate(partners, axis=0)
    coarse_rows = jnp.concatenate([own_panel, partner_rows], axis=0)

    def attention(query_all, window_all, coarse_all):
        return local_attention(query_all, window_all, window_bias, coarse_all)

    heads_out, pull = jax.vjp(
        attention, queries.astype(jnp.float32), extended.astype(jnp.float32), coarse_rows
    )
    mixed_out = lax.psum_scatter(
        jnp.dot(heads_out, out_weight, preferred_element_type=jnp.float32).astype(jnp.bfloat16),
        "head",
        scatter_dimension=0,
        tiled=True,
    )
    head_grad = lax.dot_general(
        cotangent, out_weight, (((1,), (1,)), ((), ())), preferred_element_type=jnp.float32
    ).astype(jnp.bfloat16)
    query_grad, window_grad, coarse_grad = pull(head_grad)
    rims = jnp.concatenate([window_grad[:BLOCK], window_grad[-BLOCK:]], axis=0)
    landed = extended_2(rims.astype(jnp.bfloat16), (("seq", 0),), BLOCK).astype(rims.dtype)
    inner_grad = window_grad[BLOCK : BLOCK + frame_count]
    inner_grad = inner_grad.at[:BLOCK].add(landed[:BLOCK]).at[-BLOCK:].add(landed[-BLOCK:])
    partner_grad = coarse_grad[POOL_ROWS:]
    carried = jnp.zeros_like(own_panel)
    for bit_index in reversed(range(bit_total)):
        level_grad = partner_grad[bit_index * POOL_ROWS : (bit_index + 1) * POOL_ROWS]
        upper_side = jnp.right_shift(position, bit_index) & 1 == 1
        lower_grad = pair_spread(carried[: POOL_ROWS // 2])
        upper_grad = pair_spread(carried[POOL_ROWS // 2 :])
        own_part = jnp.where(upper_side, upper_grad, lower_grad)
        level_grad = level_grad + jnp.where(upper_side, lower_grad, upper_grad)
        carried = own_part + from_partner(level_grad.astype(jnp.bfloat16), "seq", bit_index).astype(
            level_grad.dtype
        )
    panel_grad = coarse_grad[:POOL_ROWS] + carried
    spread_grad = jnp.broadcast_to(
        panel_grad[:, None, :] / math.sqrt(pool_span), (POOL_ROWS, pool_span, 2 * feature_width)
    ).reshape(frame_count, 2 * feature_width)
    total_grad = inner_grad + spread_grad
    return (
        mixed_out,
        query_grad.astype(jnp.bfloat16),
        total_grad[:, :feature_width].astype(jnp.bfloat16),
        total_grad[:, feature_width:].astype(jnp.bfloat16),
    )


def solution(mesh):
    placed = (P("seq", "head"), P("seq", "head"), P("seq", "head"), P("head", None), P("seq", None))
    return jax.shard_map(
        body,
        mesh=mesh,
        in_specs=placed,
        out_specs=(P(("seq", "head"), None), P("seq", "head"), P("seq", "head"), P("seq", "head")),
        check_vma=False,
    )
```

profile of v0, /device:TPU:0, one launch (start us, length us, event | category | flops | bytes accessed | tf_op | source)
XLA Modules:
  0.0 82.0 jit_solution(5293157863899575142)
XLA Ops:
  7.2 1.0 %constant_dynamic-update-slice_fusion.1 = bf16[256,512]{1,0:T(8,128)(2,1)S(1)} fusion(bf16[256,256]{1,0:T(8,128)(2,1)} %param.10), kind=kLoop, calls=%fused_computation.124 | loop fusion | bytes 262144
  8.2 0.9 %constant_dynamic-update-slice_fusion = bf16[256,512]{1,0:T(8,128)(2,1)S(1)} fusion(bf16[256,512]{1,0:T(8,128)(2,1)S(1)} %constant_dynamic-update-slice_fusion.1, bf16[256,256]{1,0:T(8,128)(2,1)} %param.11), kind=kLoop, calls=%fused_computation.123 | loop fusion | bytes 262144 | tf_op jit(solution)/shard_map/concatenate | solution.py:112
  9.2 4.9 %collective-permute-start = (bf16[128,512]{1,0:T(8,128)(2,1)S(1)}, bf16[128,512]{1,0:T(8,128)(2,1)S(1)}, u32[]{:S(2)}, u32[]{:S(2)}) collective-permute-start(bf16[128,512]{1,0:T(8,128)(2,1)S(1)} %get-tuple-element.164), channel_id=1, source_target_pairs={{0,4},{4,8},{8,12},{12,16},{16,20},{20,24},{24,28},{1,5},{5,9},{9,... | collective-permute-start | bytes 393224 | tf_op jit(solution)/shard_map/ppermute | solution.py:24
  14.1 1.4 %collective-permute-start.1 = (bf16[128,512]{1,0:T(8,128)(2,1)S(1)}, bf16[128,512]{1,0:T(8,128)(2,1)S(1)}, u32[]{:S(2)}, u32[]{:S(2)}) collective-permute-start(bf16[128,512]{1,0:T(8,128)(2,1)S(1)} %get-tuple-element.165), channel_id=1, source_target_pairs={{4,0},{8,4},{12,8},{16,12},{20,16},{24,20},{28,24},{5,1},{9,5},{13... | collective-permute-start | bytes 393224 | tf_op jit(solution)/shard_map/ppermute | solution.py:26
  15.5 0.2 reshape.234
  15.7 0.3 reduce_sum.58
  16.0 2.7 %collective-permute-start.2 = (f32[64,512]{1,0:T(8,128)S(1)}, f32[64,512]{1,0:T(8,128)S(1)}, u32[]{:S(2)}, u32[]{:S(2)}) collective-permute-start(f32[64,512]{1,0:T(8,128)S(1)} %broadcast_multiply_fusion), channel_id=1, source_target_pairs={{0,4},{4,0},{8,12},{12,8},{16,20},{20,16},{24,28},{28,24},{1,5},{5... | collective-permute-start | bytes 393224 | tf_op jit(solution)/shard_map/ppermute | solution.py:40
  18.7 0.3 convolution_convert_fusion.5
  19.1 0.2 copy.174
  19.3 0.1 copy.176
  19.5 0.1 copy.195
  19.6 2.8 %collective-permute-done.1 = bf16[128,512]{1,0:T(8,128)(2,1)S(1)} collective-permute-done((bf16[128,512]{1,0:T(8,128)(2,1)S(1)}, bf16[128,512]{1,0:T(8,128)(2,1)S(1)}, u32[]{:S(2)}, u32[]{:S(2)}) %collective-permute-start.1) | collective-permute-done | bytes 131104 | tf_op jit(solution)/shard_map/ppermute | solution.py:26
  22.5 0.2 copy.175
  22.7 0.2 copy.173
  22.9 1.0 %collective-permute-done.2 = f32[64,512]{1,0:T(8,128)S(1)} collective-permute-done((f32[64,512]{1,0:T(8,128)S(1)}, f32[64,512]{1,0:T(8,128)S(1)}, u32[]{:S(2)}, u32[]{:S(2)}) %collective-permute-start.2) | collective-permute-done | bytes 131104 | tf_op jit(solution)/shard_map/ppermute | solution.py:40
  24.0 0.1 fusion.77
  24.3 2.1 %collective-permute-start.3 = (f32[64,512]{1,0:T(8,128)S(1)}, f32[64,512]{1,0:T(8,128)S(1)}, u32[]{:S(2)}, u32[]{:S(2)}) collective-permute-start(f32[64,512]{1,0:T(8,128)S(1)} %pad_maximum_fusion.7), channel_id=1, source_target_pairs={{0,8},{8,0},{4,12},{12,4},{16,24},{24,16},{20,28},{28,20},{1,9},{9... | collective-permute-start | bytes 393224 | tf_op jit(solution)/shard_map/ppermute | solution.py:40
  26.4 0.1 pad_maximum_fusion
  26.5 0.8 %fusion.71 = (bf16[2,384,256]{1,2,0:T(8,128)(2,1)S(1)}, bf16[2,384,256]{1,2,0:T(8,128)(2,1)}) fusion(bf16[2,384,512]{1,2,0:T(8,128)(2,1)S(1)} %pad_maximum_fusion), kind=kLoop, calls=%fused_computation.138 | loop fusion | bytes 1572864 | tf_op jit(solution)/shard_map/slice | solution.py:51
  27.3 2.2 %collective-permute-done.3 = f32[64,512]{1,0:T(8,128)S(1)} collective-permute-done((f32[64,512]{1,0:T(8,128)S(1)}, f32[64,512]{1,0:T(8,128)S(1)}, u32[]{:S(2)}, u32[]{:S(2)}) %collective-permute-start.3) | collective-permute-done | bytes 131104 | tf_op jit(solution)/shard_map/ppermute | solution.py:40
  29.7 0.1 fusion.76
  29.9 0.1 fusion.75
  30.0 2.9 %collective-permute-start.4 = (bf16[64,512]{1,0:T(8,128)(2,1)S(1)}, bf16[64,512]{1,0:T(8,128)(2,1)S(1)}, u32[]{:S(2)}, u32[]{:S(2)}) collective-permute-start(bf16[64,512]{1,0:T(8,128)(2,1)S(1)} %pad_maximum_fusion.8), channel_id=1, source_target_pairs={{0,16},{16,0},{4,20},{20,4},{8,24},{24,8},{12,28},{28,12},{1,17},{... | collective-permute-start | bytes 196616 | tf_op jit(solution)/shard_map/ppermute | solution.py:40
  32.9 0.5 bitcast_reduce_fusion
  33.4 1.8 %collective-permute-done.4 = bf16[64,512]{1,0:T(8,128)(2,1)S(1)} collective-permute-done((bf16[64,512]{1,0:T(8,128)(2,1)S(1)}, bf16[64,512]{1,0:T(8,128)(2,1)S(1)}, u32[]{:S(2)}, u32[]{:S(2)}) %collective-permute-start.4) | collective-permute-done | bytes 65568 | tf_op jit(solution)/shard_map/ppermute | solution.py:40
  35.3 0.7 fusion.73
  36.1 0.4 bitcast_reduce_fusion.1
  36.5 0.2 fusion.28
  36.7 0.2 fusion.29
  36.9 0.6 copy.199
  37.5 0.6 copy.192
  38.1 1.6 %fusion.1 = (f32[2,4,128]{2,1,0:T(4,128)S(1)}, bf16[2,4,128,384]{2,3,1,0:T(8,128)(2,1)S(1)}, bf16[2,4,128,384]{2,3,1,0:T(8,128)(2,1)}) fusion(f32[2,4,384,128]{3,2,1,0:T(8,128)S(1)} %get-tuple-element.183, f32[2,4,128]{2,1,0:T(4,128)S(1)} %get-tuple-element.141, f32[2,4,128]{2,1,0:T(4,128)S(1)} %copy_maximum_fusion, ...), kind=kOutput, calls=%fused_computation.3 | convolution fusion | flops 53476352 | bytes 3686400 | tf_op jit(solution)/shard_map/transpose(jvp())/while/body/eval_jaxpr/nhqk,nkhd->nqhd/dot_general | solution.py:75
  39.7 1.0 %convolution_bitcast_fusion.3 = f32[2,128,4,64]{1,3,2,0:T(8,128)} fusion(bf16[2,384,4,64]{1,3,2,0:T(8,128)(2,1)S(1)} %bitcast.145, bf16[2,4,128,384]{2,3,1,0:T(8,128)(2,1)S(1)} %get-tuple-element.144), kind=kOutput, calls=%fused_computation.26 | convolution fusion | flops 50331648 | bytes 1441792 | tf_op jit(solution)/shard_map/nhqk,nkhd->nqhd/dot_general | solution.py:75
  40.7 1.2 %convolution_convert_fusion.4 = bf16[2,4,64,384]{3,2,1,0:T(8,128)(2,1)} fusion(bf16[2,4,128,384]{2,3,1,0:T(8,128)(2,1)S(1)} %get-tuple-element.144, bf16[2,4,64,128]{3,0,2,1:T(2,128)(2,1)S(1)} %bitcast.147), kind=kOutput, calls=%fused_computation.21 | convolution fusion | flops 50528256 | bytes 1310720 | tf_op jit(solution)/shard_map/transpose(jvp())/while/body/eval_jaxpr/nhqk,nkhd->nqhd/dot_general | solution.py:75
  41.9 0.8 copy.191
  42.7 2.4 %fusion.26 = (f32[2,4,128]{2,0,1:T(2,128)S(1)}, bf16[2,4,128,256]{2,3,0,1:T(8,128)(2,1)}, bf16[4,2,128,256]{2,3,1,0:T(8,128)(2,1)}) fusion(f32[4,256,2,128]{3,1,2,0:T(8,128)S(1)} %get-tuple-element.185, f32[2,4,128]{2,0,1:T(2,128)} %copy.199, f32[2,4,128]{2,0,1:T(2,128)S(1)} %copy.188, f32[2,4,128]{2,0,1:T(2,128)} %copy.192, ...), kind=kOutput, calls=%fused_computation.42 | convolution fusion | flops 35650560 | bytes 2375680 | tf_op jit(solution)/shard_map/transpose(jvp())/while/body/eval_jaxpr/nhqk,khd->nqhd/dot_general | solution.py:78
  45.1 0.5 fusion.4
  45.6 0.5 copy-done.3
  46.1 0.9 %fusion.17 = bf16[2,128,4,64]{1,3,0,2:T(8,128)(2,1)} fusion(bf16[2,4,128,384]{2,3,1,0:T(8,128)(2,1)S(1)} %fusion.4, bf16[2,384,4,64]{1,3,2,0:T(8,128)(2,1)S(1)} %bitcast.141), kind=kOutput, calls=%fused_computation.35 | convolution fusion | flops 50331648 | bytes 1310720 | tf_op jit(solution)/shard_map/transpose(jvp())/while/body/eval_jaxpr/nqhd,nkhd->nhqk/dot_general | solution.py:59
  47.1 0.5 convolution_convert_fusion.3
  47.5 0.2 copy.210
  47.7 0.2 copy.213
  48.0 1.1 %fusion.70 = (f32[4,128,512]{2,1,0:T(8,128)}, bf16[4,128,512]{2,1,0:T(8,128)(2,1)S(1)}) fusion(bf16[2,128,512]{2,1,0:T(8,128)(2,1)S(1)} %get-tuple-element.148, bf16[2,128,512]{2,1,0:T(8,128)(2,1)S(1)} %get-tuple-element.149, bf16[2,128,512]{2,1,0:T(8,128)(2,1)S(1)} %get-tuple-element.147), kind=kLoop, calls=%fused_computation.137 | loop fusion | flops 786432 | bytes 2359296 | tf_op jit(solution)/shard_map/transpose(jvp())/while/body/eval_jaxpr/convert_element_type | solution.py:49
  49.2 0.7 slice_bitcast_fusion.2
  49.8 0.3 fusion.11
  50.2 0.2 fusion.10
  50.4 0.1 copy.194
  50.5 1.1 %convolution_convert_fusion.1 = bf16[256,1024]{1,0:T(8,128)(2,1)} fusion(bf16[256,1024]{1,0:T(8,128)(2,1)S(1)} %copy-done, bf16[32,8,2,128]{3,2,1,0:T(2,128)(2,1)S(1)} %bitcast.154), kind=kOutput, calls=%fused_computation.18 | convolution fusion | flops 134479872 | bytes 1179648 | tf_op jit(solution)/shard_map/dot_general | solution.py:142
  51.7 0.4 fusion.9
  52.2 0.1 copy.218
  52.3 0.1 copy.216
  52.4 2.9 %collective-permute-start.7 = (bf16[64,512]{1,0:T(8,128)(2,1)S(1)}, bf16[64,512]{1,0:T(8,128)(2,1)S(1)}, u32[]{:S(2)}, u32[]{:S(2)}) collective-permute-start(bf16[64,512]{1,0:T(8,128)(2,1)S(1)} %fusion.50), channel_id=1, source_target_pairs={{0,16},{16,0},{4,20},{20,4},{8,24},{24,8},{12,28},{28,12},{1,17},{... | collective-permute-start | bytes 196616 | tf_op jit(solution)/shard_map/ppermute | solution.py:40
  55.4 2.4 %collective-permute-done.7 = bf16[64,512]{1,0:T(8,128)(2,1)S(1)} collective-permute-done((bf16[64,512]{1,0:T(8,128)(2,1)S(1)}, bf16[64,512]{1,0:T(8,128)(2,1)S(1)}, u32[]{:S(2)}, u32[]{:S(2)}) %collective-permute-start.7) | collective-permute-done | bytes 65568 | tf_op jit(solution)/shard_map/ppermute | solution.py:40
  58.0 2.0 %collective-permute-start.8 = (bf16[64,512]{1,0:T(8,128)(2,1)S(1)}, bf16[64,512]{1,0:T(8,128)(2,1)S(1)}, u32[]{:S(2)}, u32[]{:S(2)}) collective-permute-start(bf16[64,512]{1,0:T(8,128)(2,1)S(1)} %fusion.40), channel_id=1, source_target_pairs={{0,8},{8,0},{4,12},{12,4},{16,24},{24,16},{20,28},{28,20},{1,9},{9... | collective-permute-start | bytes 196616 | tf_op jit(solution)/shard_map/ppermute | solution.py:40
  60.0 1.5 %fusion.16 = bf16[2,128,4,64]{1,3,0,2:T(8,128)(2,1)S(1)} fusion(bf16[2,128,4,64]{1,3,0,2:T(8,128)(2,1)S(1)} %copy-done.15, bf16[256,4,64,1]{0,2,3,1:T(8,128)(2,1)S(1)} %bitcast.153, bf16[4,2,128,256]{2,3,1,0:T(8,128)(2,1)} %get-tuple-element.187, f32[4,256,2,128]{3,1,2,0:T(8,128)S(1)} %get-tuple-element.185, f32[4,2,128]{2,1,0:T(2,128)S(1)} %copy.204, ...), kind=kOutput, calls=%fused_computation.34 | convolution fusion | flops 35258368 | bytes 1978368 | tf_op jit(solution)/shard_map/transpose(jvp())/while/body/eval_jaxpr/nqhd,khd->nhqk/dot_general | solution.py:64
  61.5 0.2 copy.236
  61.7 0.9 %reshape.239 = bf16[256,256]{1,0:T(8,128)(2,1)} reshape(bf16[2,128,4,64]{3,2,1,0:T(4,128)(2,1)S(1)} %copy.236) | data formatting | bytes 262144
  62.6 1.3 %collective-permute-start.6 = (bf16[128,512]{1,0:T(8,128)(2,1)S(1)}, bf16[128,512]{1,0:T(8,128)(2,1)S(1)}, u32[]{:S(2)}, u32[]{:S(2)}) collective-permute-start(bf16[128,512]{1,0:T(8,128)(2,1)S(1)} %copy-done.6), channel_id=1, source_target_pairs={{4,0},{8,4},{12,8},{16,12},{20,16},{24,20},{28,24},{5,1},{9,5},{13... | collective-permute-start | bytes 393224 | tf_op jit(solution)/shard_map/ppermute | solution.py:26
  63.9 4.6 %collective-permute-start.5 = (bf16[128,512]{1,0:T(8,128)(2,1)S(1)}, bf16[128,512]{1,0:T(8,128)(2,1)S(1)}, u32[]{:S(2)}, u32[]{:S(2)}) collective-permute-start(bf16[128,512]{1,0:T(8,128)(2,1)S(1)} %get-tuple-element.152), channel_id=1, source_target_pairs={{0,4},{4,8},{8,12},{12,16},{16,20},{20,24},{24,28},{1,5},{5,9},{9,... | collective-permute-start | bytes 393224 | tf_op jit(solution)/shard_map/ppermute | solution.py:24
  68.8 3.0 %collective-permute-start.9 = (bf16[64,512]{1,0:T(8,128)(2,1)S(1)}, bf16[64,512]{1,0:T(8,128)(2,1)S(1)}, u32[]{:S(2)}, u32[]{:S(2)}) collective-permute-start(bf16[64,512]{1,0:T(8,128)(2,1)S(1)} %fusion.39), channel_id=1, source_target_pairs={{0,4},{4,0},{8,12},{12,8},{16,20},{20,16},{24,28},{28,24},{1,5},{5... | collective-permute-start | bytes 196616 | tf_op jit(solution)/shard_map/ppermute | solution.py:40
  71.8 1.0 %fusion.36 = f32[256,512]{1,0:T(8,128)S(1)} fusion(f32[256,512]{1,0:T(8,128)S(1)} %bitcast.139, f32[4,128,512]{2,1,0:T(8,128)} %get-tuple-element.139, bf16[128,512]{1,0:T(8,128)(2,1)S(1)} %collective-permute-done.6, bf16[128,512]{1,0:T(8,128)(2,1)S(1)} %get-tuple-element.152, bf16[128,512]{1,0:T(8,128)(2,1)S(1)} %copy-done.6, ...), kind=kLoop, calls=%fused_computation.67 | loop fusion | flops 589824 | bytes 1048576 | tf_op jit(solution)/shard_map/scatter-add | solution.py:154
  73.0 1.0 %collective-permute-done.9 = bf16[64,512]{1,0:T(8,128)(2,1)S(1)} collective-permute-done((bf16[64,512]{1,0:T(8,128)(2,1)S(1)}, bf16[64,512]{1,0:T(8,128)(2,1)S(1)}, u32[]{:S(2)}, u32[]{:S(2)}) %collective-permute-start.9) | collective-permute-done | bytes 65568 | tf_op jit(solution)/shard_map/ppermute | solution.py:40
  74.1 0.2 reshape.233
  74.4 0.7 fusion.72
  (91 shorter events, 2.1 us)
Async XLA Ops:
  7.2 11.6 %copy-start = (bf16[256,1024]{1,0:T(8,128)(2,1)S(1)}, bf16[256,1024]{1,0:T(8,128)(2,1)}, u32[]{:S(2)}) copy-start(bf16[256,1024]{1,0:T(8,128)(2,1)} %param.12) | copy-start | bytes 1572868
  7.2 11.6 %copy-start.11 = (bf16[256,1024]{1,0:T(8,128)(2,1)S(1)}, bf16[256,1024]{1,0:T(8,128)(2,1)}, u32[]{:S(2)}) copy-start(bf16[256,1024]{1,0:T(8,128)(2,1)} %param.13) | copy-start | bytes 1572868
  7.2 68.0 %reduce-scatter.2.cloned.1.call-start = ((), (), s32[]{:S(2)}) async-start(), calls=%async_computation.1 | async-start | bytes 655360 | tf_op jit(solution)/shard_map/reduce_scatter | solution.py:141
  9.2 10.4 %collective-permute-start = (bf16[128,512]{1,0:T(8,128)(2,1)S(1)}, bf16[128,512]{1,0:T(8,128)(2,1)S(1)}, u32[]{:S(2)}, u32[]{:S(2)}) collective-permute-start(bf16[128,512]{1,0:T(8,128)(2,1)S(1)} %get-tuple-element.164), channel_id=1, source_target_pairs={{0,4},{4,8},{8,12},{12,16},{16,20},{20,24},{24,28},{1,5},{5,9},{9,... | collective-permute-start | bytes 393224 | tf_op jit(solution)/shard_map/ppermute | solution.py:24
  14.1 5.2 %copy-start.14 = (bf16[256,256]{1,0:T(8,128)(2,1)S(1)}, bf16[256,256]{1,0:T(8,128)(2,1)}, u32[]{:S(2)}) copy-start(bf16[256,256]{1,0:T(8,128)(2,1)} %param.9) | copy-start | bytes 393220
  14.1 8.4 %collective-permute-start.1 = (bf16[128,512]{1,0:T(8,128)(2,1)S(1)}, bf16[128,512]{1,0:T(8,128)(2,1)S(1)}, u32[]{:S(2)}, u32[]{:S(2)}) collective-permute-start(bf16[128,512]{1,0:T(8,128)(2,1)S(1)} %get-tuple-element.165), channel_id=1, source_target_pairs={{4,0},{8,4},{12,8},{16,12},{20,16},{24,20},{28,24},{5,1},{9,5},{13... | collective-permute-start | bytes 393224 | tf_op jit(solution)/shard_map/ppermute | solution.py:26
  16.0 7.8 %collective-permute-start.2 = (f32[64,512]{1,0:T(8,128)S(1)}, f32[64,512]{1,0:T(8,128)S(1)}, u32[]{:S(2)}, u32[]{:S(2)}) collective-permute-start(f32[64,512]{1,0:T(8,128)S(1)} %broadcast_multiply_fusion), channel_id=1, source_target_pairs={{0,4},{4,0},{8,12},{12,8},{16,20},{20,16},{24,28},{28,24},{1,5},{5... | collective-permute-start | bytes 393224 | tf_op jit(solution)/shard_map/ppermute | solution.py:40
  24.3 5.2 %collective-permute-start.3 = (f32[64,512]{1,0:T(8,128)S(1)}, f32[64,512]{1,0:T(8,128)S(1)}, u32[]{:S(2)}, u32[]{:S(2)}) collective-permute-start(f32[64,512]{1,0:T(8,128)S(1)} %pad_maximum_fusion.7), channel_id=1, source_target_pairs={{0,8},{8,0},{4,12},{12,4},{16,24},{24,16},{20,28},{28,20},{1,9},{9... | collective-permute-start | bytes 393224 | tf_op jit(solution)/shard_map/ppermute | solution.py:40
  27.3 6.1 %copy-start.2 = (bf16[2,384,256]{1,2,0:T(8,128)(2,1)}, bf16[2,384,256]{1,2,0:T(8,128)(2,1)S(1)}, u32[]{:S(2)}) copy-start(bf16[2,384,256]{1,2,0:T(8,128)(2,1)S(1)} %get-tuple-element.150) | copy-start | bytes 1179652
  30.0 5.2 %collective-permute-start.4 = (bf16[64,512]{1,0:T(8,128)(2,1)S(1)}, bf16[64,512]{1,0:T(8,128)(2,1)S(1)}, u32[]{:S(2)}, u32[]{:S(2)}) collective-permute-start(bf16[64,512]{1,0:T(8,128)(2,1)S(1)} %pad_maximum_fusion.8), channel_id=1, source_target_pairs={{0,16},{16,0},{4,20},{20,4},{8,24},{24,8},{12,28},{28,12},{1,17},{... | collective-permute-start | bytes 196616 | tf_op jit(solution)/shard_map/ppermute | solution.py:40
  36.1 0.8 copy-start.9
  36.4 1.7 %copy-start.5 = (bf16[2,384,256]{1,2,0:T(8,128)(2,1)S(1)}, bf16[2,384,256]{1,2,0:T(8,128)(2,1)}, u32[]{:S(2)}) copy-start(bf16[2,384,256]{1,2,0:T(8,128)(2,1)} %get-tuple-element.151) | copy-start | bytes 1179652
  39.7 2.2 %copy-start.12 = (bf16[256,256]{1,0:T(8,128)(2,1)S(1)}, bf16[256,256]{1,0:T(8,128)(2,1)}, u32[]{:S(2)}) copy-start(bf16[256,256]{1,0:T(8,128)(2,1)} %get-tuple-element.156) | copy-start | bytes 393220
  42.7 2.4 %copy-start.8 = (bf16[2,4,128,384]{2,3,1,0:T(8,128)(2,1)S(1)}, bf16[2,4,128,384]{2,3,1,0:T(8,128)(2,1)}, u32[]{:S(2)}) copy-start(bf16[2,4,128,384]{2,3,1,0:T(8,128)(2,1)} %get-tuple-element.186) | copy-start | bytes 2359300
  45.1 1.0 %copy-start.3 = (bf16[2,384,256]{1,2,0:T(8,128)(2,1)S(1)}, bf16[2,384,256]{1,2,0:T(8,128)(2,1)}, u32[]{:S(2)}) copy-start(bf16[2,384,256]{1,2,0:T(8,128)(2,1)} %copy-done.2) | copy-start | bytes 1179652
  46.1 1.4 %copy-start.4 = (bf16[2,4,64,384]{3,2,1,0:T(8,128)(2,1)S(1)}, bf16[2,4,64,384]{3,2,1,0:T(8,128)(2,1)}, u32[]{:S(2)}) copy-start(bf16[2,4,64,384]{3,2,1,0:T(8,128)(2,1)} %convolution_convert_fusion.4) | copy-start | bytes 1179652
  48.0 1.9 %copy-start.1 = (bf16[2,4,128,256]{2,3,0,1:T(8,128)(2,1)S(1)}, bf16[2,4,128,256]{2,3,0,1:T(8,128)(2,1)}, u32[]{:S(2)}) copy-start(bf16[2,4,128,256]{2,3,0,1:T(8,128)(2,1)} %get-tuple-element.146) | copy-start | bytes 1572868
  49.1 1.0 %copy-start.7 = (f32[2,128,4,64]{1,3,2,0:T(8,128)S(1)}, f32[2,128,4,64]{1,3,2,0:T(8,128)}, u32[]{:S(2)}) copy-start(f32[2,128,4,64]{1,3,2,0:T(8,128)} %convolution_bitcast_fusion.3) | copy-start | bytes 786436
  49.1 1.0 %copy-start.13 = (bf16[256,256]{0,1:T(8,128)(2,1)S(1)}, bf16[256,256]{0,1:T(8,128)(2,1)}, u32[]{:S(2)}) copy-start(bf16[256,256]{0,1:T(8,128)(2,1)} %copy.191) | copy-start | bytes 393220
  50.1 1.6 %copy-start.16 = (bf16[4,2,128,256]{2,3,1,0:T(8,128)(2,1)S(1)}, bf16[4,2,128,256]{2,3,1,0:T(8,128)(2,1)}, u32[]{:S(2)}) copy-start(bf16[4,2,128,256]{2,3,1,0:T(8,128)(2,1)} %get-tuple-element.187) | copy-start | bytes 1572868
  52.2 7.8 %copy-start.10 = (bf16[256,256]{0,1:T(8,128)(2,1)S(1)}, bf16[256,256]{0,1:T(8,128)(2,1)}, u32[]{:S(2)}) copy-start(bf16[256,256]{0,1:T(8,128)(2,1)} %copy-done.9) | copy-start | bytes 393220
  52.2 7.8 %copy-start.15 = (bf16[2,128,4,64]{1,3,0,2:T(8,128)(2,1)S(1)}, bf16[2,128,4,64]{1,3,0,2:T(8,128)(2,1)}, u32[]{:S(2)}) copy-start(bf16[2,128,4,64]{1,3,0,2:T(8,128)(2,1)} %fusion.17) | copy-start | bytes 393220
  52.4 5.4 %collective-permute-start.7 = (bf16[64,512]{1,0:T(8,128)(2,1)S(1)}, bf16[64,512]{1,0:T(8,128)(2,1)S(1)}, u32[]{:S(2)}, u32[]{:S(2)}) collective-permute-start(bf16[64,512]{1,0:T(8,128)(2,1)S(1)} %fusion.50), channel_id=1, source_target_pairs={{0,16},{16,0},{4,20},{20,4},{8,24},{24,8},{12,28},{28,12},{1,17},{... | collective-permute-start | bytes 196616 | tf_op jit(solution)/shard_map/ppermute | solution.py:40
  58.0 4.6 %copy-start.6 = (bf16[128,512]{1,0:T(8,128)(2,1)S(1)}, bf16[128,512]{1,0:T(8,128)(2,1)}, u32[]{:S(2)}) copy-start(bf16[128,512]{1,0:T(8,128)(2,1)} %get-tuple-element.153) | copy-start | bytes 393220
  58.0 10.6 %collective-permute-start.8 = (bf16[64,512]{1,0:T(8,128)(2,1)S(1)}, bf16[64,512]{1,0:T(8,128)(2,1)S(1)}, u32[]{:S(2)}, u32[]{:S(2)}) collective-permute-start(bf16[64,512]{1,0:T(8,128)(2,1)S(1)} %fusion.40), channel_id=1, source_target_pairs={{0,8},{8,0},{4,12},{12,4},{16,24},{24,16},{20,28},{28,20},{1,9},{9... | collective-permute-start | bytes 196616 | tf_op jit(solution)/shard_map/ppermute | solution.py:40
  62.6 9.2 %collective-permute-start.6 = (bf16[128,512]{1,0:T(8,128)(2,1)S(1)}, bf16[128,512]{1,0:T(8,128)(2,1)S(1)}, u32[]{:S(2)}, u32[]{:S(2)}) collective-permute-start(bf16[128,512]{1,0:T(8,128)(2,1)S(1)} %copy-done.6), channel_id=1, source_target_pairs={{4,0},{8,4},{12,8},{16,12},{20,16},{24,20},{28,24},{5,1},{9,5},{13... | collective-permute-start | bytes 393224 | tf_op jit(solution)/shard_map/ppermute | solution.py:26
  63.9 7.9 %collective-permute-start.5 = (bf16[128,512]{1,0:T(8,128)(2,1)S(1)}, bf16[128,512]{1,0:T(8,128)(2,1)S(1)}, u32[]{:S(2)}, u32[]{:S(2)}) collective-permute-start(bf16[128,512]{1,0:T(8,128)(2,1)S(1)} %get-tuple-element.152), channel_id=1, source_target_pairs={{0,4},{4,8},{8,12},{12,16},{16,20},{20,24},{24,28},{1,5},{5,9},{9,... | collective-permute-start | bytes 393224 | tf_op jit(solution)/shard_map/ppermute | solution.py:24
  68.8 5.2 %collective-permute-start.9 = (bf16[64,512]{1,0:T(8,128)(2,1)S(1)}, bf16[64,512]{1,0:T(8,128)(2,1)S(1)}, u32[]{:S(2)}, u32[]{:S(2)}) collective-permute-start(bf16[64,512]{1,0:T(8,128)(2,1)S(1)} %fusion.39), channel_id=1, source_target_pairs={{0,4},{4,0},{8,12},{12,8},{16,20},{20,16},{24,28},{28,24},{1,5},{5... | collective-permute-start | bytes 196616 | tf_op jit(solution)/shard_map/ppermute | solution.py:40
Sparse Core Ops, SparseCore 0:
  51.8 22.8 reduce-scatter.1
where the time goes:
time: 82.4 us; the launch traced here: 82 us
  starting transfers between devices  27.7 us (34%)
  between operations  14.8 us (18%)
  matrix products  12.4 us (15%)
  local copies, waits for them, and re-layouts  11.7 us (14%)
  waiting for transfers between devices  11.3 us (14%)
  other arithmetic  4.09 us (5%)
    ppermute x6, starting transfers between devices, from_partner(): return lax.ppermute(block, axis, route)  15.5 us
    ppermute x2, starting transfers between devices, extended_2(): lax.ppermute(tail, axis, [(i, (i + 1) % count) for i in range(ends)])  9.43 us
    ppermute x6, waiting for transfers between devices, from_partner(): return lax.ppermute(block, axis, route)  8.48 us
    dot_general x3, matrix products, attend(): jnp.einsum('nhqk,nkhd->nqhd', fine_weights, fine_values, preferred_elemen...  3.82 us
    dot_general x3, matrix products, attend(): jnp.einsum('nhqk,khd->nqhd', coarse_weights, coarse_values, preferred_ele...  2.93 us
    ppermute x2, waiting for transfers between devices, extended_2(): lax.ppermute(head, axis, [((i + 1) % count, i) for i in range(ends)])  2.85 us
    unnamed x38, local copies, waits for them, and re-layouts  2.75 us
    ppermute x2, starting transfers between devices, extended_2(): lax.ppermute(head, axis, [((i + 1) % count, i) for i in range(ends)])  2.7 us
  transfers between devices with their start and end apart: 11, of which 6 were waited for; matrix products, arithmetic and copies ran while one was open for 11% of the time, Pallas kernels for 0%

commit v1 on v0

v1 whole, which is shorter than its diff:
```python
import functools
import math

import jax
import jax.numpy as jnp
from jax import lax
from jax.experimental import pallas as pl
from jax.experimental.pallas import tpu as pltpu
from jax.sharding import PartitionSpec as P

HEAD_DIM = 64
PAIR = 2 * HEAD_DIM
BLOCK = 128
POOL_ROWS = 64
MIN_SLOT = 16
MASKED = -1000000000.0
MESH = pl.DeviceIdType.MESH
F32 = jnp.float32
BF16 = jnp.bfloat16


def dot_nn(a, b):
    return lax.dot_general(a, b, (((1,), (0,)), ((), ())), preferred_element_type=F32)


def dot_nt(a, b):
    return lax.dot_general(a, b, (((1,), (1,)), ((), ())), preferred_element_type=F32)


def dot_tn(a, b):
    return lax.dot_general(a, b, (((0,), (0,)), ((), ())), preferred_element_type=F32)


class Plan:
    def __init__(self, n_seq, frames):
        self.bits = n_seq.bit_length() - 1
        self.span = frames // POOL_ROWS
        self.rows = [POOL_ROWS >> b for b in range(self.bits)]
        self.slot = [max(MIN_SLOT, r) for r in self.rows]
        self.send_at, at = [], 0
        for b in range(self.bits):
            self.send_at.append(at)
            at += self.slot[b]
        self.send_rows = at
        self.coarse_rows = POOL_ROWS * (1 + self.bits)
        self.direct = [r >= MIN_SLOT for r in self.rows]
        self.wide_at, at = {}, 0
        for b in range(self.bits):
            if not self.direct[b]:
                self.wide_at[b] = at
                at += self.slot[b] << b
        self.wide_rows = max(at, MIN_SLOT)
        self.grad_at, at = {"own": 0}, POOL_ROWS
        for b in range(0, self.bits, 2):
            self.grad_at[b] = at
            at += self.slot[b] << b
        self.even_rows = at
        for b in range(1, self.bits, 2):
            self.grad_at[b] = at
            at += self.slot[b] << b
        self.grad_rows = at


def flip(me, m):
    out, b = me, 0
    while m >> b:
        if (m >> b) & 1:
            out = out + (1 << b) * (1 - 2 * (me // (1 << b) % 2))
        b += 1
    return out


def pool_matrix(plan, frames):
    row = lax.broadcasted_iota(jnp.int32, (plan.send_rows, frames), 0)
    col = lax.broadcasted_iota(jnp.int32, (plan.send_rows, frames), 1)
    hit = None
    for b in range(plan.bits):
        width = plan.span << b
        lo = plan.send_at[b]
        rel = col - (row - lo) * width
        now = (row >= lo) & (row < lo + plan.slot[b]) & (rel >= 0) & (rel < width)
        hit = now if hit is None else hit | now
    return jnp.where(hit, 1.0, 0.0).astype(BF16)


def spread_matrix(plan, frames, levels, base, width_all):
    frame = lax.broadcasted_iota(jnp.int32, (frames, width_all), 0)
    col = lax.broadcasted_iota(jnp.int32, (frames, width_all), 1)
    out = jnp.zeros((frames, width_all), F32)
    for level in levels:
        b = 0 if level == "own" else level
        lo = plan.grad_at[level] - base
        total = POOL_ROWS if level == "own" else plan.slot[b] << b
        width = plan.span << b
        rel = frame - ((col - lo) & (plan.slot[b] - 1)) * width
        hit = (col >= lo) & (col < lo + total) & (rel >= 0) & (rel < width)
        out = jnp.where(hit, 0.5 ** (b // 2), out)
    return out.astype(BF16)


def compact_matrix(plan, b):
    total = plan.slot[b] << b
    row = lax.broadcasted_iota(jnp.int32, (POOL_ROWS, total), 0)
    col = lax.broadcasted_iota(jnp.int32, (POOL_ROWS, total), 1)
    r = plan.rows[b]
    hit = ((col // plan.slot[b]) == (row // r)) & ((col & (plan.slot[b] - 1)) == (row & (r - 1)))
    return jnp.where(hit, 1.0, 0.0).astype(BF16)


def kernel(
    n_seq,
    n_head,
    plan,
    q_hbm,
    k_hbm,
    v_hbm,
    w_hbm,
    c_hbm,
    mixed_ref,
    qg_ref,
    kg_ref,
    vg_ref,
    q_ref,
    ext,
    w_ref,
    c_ref,
    pool_send,
    coarse,
    wide,
    hgrad,
    heads,
    qstack,
    gstack,
    weights,
    delta,
    mix_send,
    mix_recv,
    rim_send,
    rim_recv,
    inner,
    cg_send,
    grad,
    load_sem,
    halo_ssem,
    halo_rsem,
    pool_ssem,
    pool_rsem,
    rim_ssem,
    rim_rsem,
    cg_ssem,
    cg_rsem,
    mix_ssem,
    mix_rsem,
):
    me = lax.axis_index("seq")
    hme = lax.axis_index("head")
    frames, feats = q_ref.shape
    blocks = frames // BLOCK
    pairs = feats // PAIR
    bits = plan.bits
    window = 3 * BLOCK

    own_rows = pl.ds(BLOCK, frames)
    loads = [
        pltpu.make_async_copy(k_hbm, ext.at[own_rows, pl.ds(0, feats)], load_sem.at[0]),
        pltpu.make_async_copy(v_hbm, ext.at[own_rows, pl.ds(feats, feats)], load_sem.at[1]),
        pltpu.make_async_copy(c_hbm, c_ref, load_sem.at[2]),
        pltpu.make_async_copy(w_hbm, w_ref, load_sem.at[3]),
        pltpu.make_async_copy(q_hbm, q_ref, load_sem.at[4]),
    ]
    for load in loads:
        load.start()

    barrier = pltpu.get_barrier_semaphore()
    for m in range(1, n_seq):
        pl.semaphore_signal(barrier, inc=1, device_id=(flip(me, m), hme), device_id_type=MESH)
    for m in range(1, n_head):
        pl.semaphore_signal(
            barrier, inc=1, device_id=(me, lax.rem(hme + m, n_head)), device_id_type=MESH
        )

    @pl.when(me == 0)
    def _():
        ext[pl.ds(0, BLOCK), :] = jnp.zeros((BLOCK, 2 * feats), BF16)
        rim_recv[0] = jnp.zeros((BLOCK, 2 * feats), BF16)

    @pl.when(me == n_seq - 1)
    def _():
        ext[pl.ds(BLOCK + frames, BLOCK), :] = jnp.zeros((BLOCK, 2 * feats), BF16)
        rim_recv[1] = jnp.zeros((BLOCK, 2 * feats), BF16)

    loads[0].wait()
    loads[1].wait()
    sums = dot_nn(pool_matrix(plan, frames), ext[own_rows, :])
    for b in range(bits):
        at = plan.send_at[b]
        level = sums[at : at + plan.slot[b]] * (1.0 / math.sqrt(plan.span << b))
        pool_send[pl.ds(at, plan.slot[b]), :] = level.astype(BF16)
        if b == 0:
            coarse[pl.ds(0, POOL_ROWS), :] = level.astype(BF16)

    pl.semaphore_wait(barrier, n_seq - 1 + n_head - 1)

    def halo(side):
        return pltpu.make_async_remote_copy(
            src_ref=ext.at[pl.ds(frames if side == 0 else BLOCK, BLOCK), :],
            dst_ref=ext.at[pl.ds(0 if side == 0 else BLOCK + frames, BLOCK), :],
            send_sem=halo_ssem.at[side],
            recv_sem=halo_rsem.at[side],
            device_id=(me + 1 if side == 0 else me - 1, hme),
            device_id_type=MESH,
        )

    pool_copies = {}
    for m in reversed(range(1, n_seq)):
        b = m.bit_length() - 1
        slot = m - (1 << b)
        if plan.direct[b]:
            landing = coarse.at[pl.ds(POOL_ROWS * (1 + b) + slot * plan.slot[b], plan.slot[b]), :]
        else:
            landing = wide.at[pl.ds(plan.wide_at[b] + slot * plan.slot[b], plan.slot[b]), :]
        copy = pltpu.make_async_remote_copy(
            src_ref=pool_send.at[pl.ds(plan.send_at[b], plan.slot[b]), :],
            dst_ref=landing,
            send_sem=pool_ssem.at[m - 1],
            recv_sem=pool_rsem.at[m - 1],
            device_id=(flip(me, m), hme),
            device_id_type=MESH,
        )
        copy.start()
        pool_copies[m] = copy

    @pl.when(me < n_seq - 1)
    def _():
        halo(0).start()

    @pl.when(me > 0)
    def _():
        halo(1).start()

    loads[2].wait()
    loads[3].wait()
    hgrad[...] = dot_nt(c_ref[...], w_ref[...]).astype(BF16)
    loads[4].wait()

    lane = lax.broadcasted_iota(jnp.int32, (BLOCK, PAIR), 1)
    first = lane < HEAD_DIM

    def stacked(block):
        zero = jnp.zeros_like(block)
        return jnp.concatenate(
            [jnp.where(first, block, zero), jnp.where(first, zero, block)], axis=0
        )

    scale = 1.0 / math.sqrt(HEAD_DIM)
    for p in range(pairs):
        for n in range(blocks):
            u = p * blocks + n
            rows, cols = pl.ds(n * BLOCK, BLOCK), pl.ds(p * PAIR, PAIR)
            qstack[u] = (stacked(q_ref[rows, cols].astype(F32)) * scale).astype(BF16)
            gstack[u] = stacked(hgrad[rows, cols].astype(F32)).astype(BF16)

    for m in range(1, n_seq):
        pool_copies[m].wait()

    @pl.when(me > 0)
    def _():
        halo(0).wait_recv()
        halo(1).wait_send()

    @pl.when(me < n_seq - 1)
    def _():
        halo(1).wait_recv()
        halo(0).wait_send()

    for b in range(bits):
        if not plan.direct[b]:
            packed = wide[pl.ds(plan.wide_at[b], plan.slot[b] << b), :]
            coarse[pl.ds(POOL_ROWS * (1 + b), POOL_ROWS), :] = dot_nn(
                compact_matrix(plan, b), packed
            ).astype(BF16)

    left_bias = jnp.where(me == 0, MASKED, 0.0).astype(F32)
    right_bias = jnp.where(me == n_seq - 1, MASKED, 0.0).astype(F32)

    def keys(p, n, side):
        cols = pl.ds(side * feats + p * PAIR, PAIR)
        return ext[pl.ds(n * BLOCK, window), cols], coarse[:, cols]

    def heads_of(both):
        return jnp.concatenate(
            [both[:HEAD_DIM, :BLOCK], both[HEAD_DIM:, BLOCK:]], axis=0
        )

    for p in range(pairs):
        for n in range(blocks):
            u = p * blocks + n
            rows, cols = pl.ds(n * BLOCK, BLOCK), pl.ds(p * PAIR, PAIR)
            kf, kc = keys(p, n, 0)
            vf, vc = keys(p, n, 1)
            qs = qstack[u]
            sf = dot_nt(kf, qs)
            sc = dot_nt(kc, qs)
            parts = [sf[i * BLOCK : (i + 1) * BLOCK] for i in range(3)]
            if n == 0:
                parts[0] = parts[0] + left_bias
            if n == blocks - 1:
                parts[2] = parts[2] + right_bias
            parts.append(sc)
            top = functools.reduce(
                jnp.maximum, [x.max(axis=0, keepdims=True) for x in parts]
            )
            parts = [jnp.exp(x - top) for x in parts]
            total = sum(x.sum(axis=0, keepdims=True) for x in parts)
            inv = 1.0 / total
            parts = [(x * inv).astype(BF16) for x in parts]
            pf = jnp.concatenate(parts[:3], axis=0)
            pc = parts[3]
            weights[u, pl.ds(0, window), :] = pf
            weights[u, pl.ds(window, plan.coarse_rows), :] = pc
            out = heads_of(dot_tn(vf, pf) + dot_tn(vc, pc))
            heads[rows, cols] = out.T.astype(BF16)
            prod = out * hgrad[rows, cols].astype(F32).T
            delta[u] = jnp.concatenate(
                [
                    prod[:HEAD_DIM].sum(axis=0, keepdims=True),
                    prod[HEAD_DIM:].sum(axis=0, keepdims=True),
                ],
                axis=1,
            )

    share = frames // n_head
    mixed = dot_nn(heads[...], w_ref[...]).astype(BF16)
    for h in range(n_head):
        mix_send[h] = mixed[h * share : (h + 1) * share]
    mix_copies = []
    for m in range(1, n_head):
        peer = lax.rem(hme + m, n_head)
        copy = pltpu.make_async_remote_copy(
            src_ref=mix_send.at[peer],
            dst_ref=mix_recv.at[m - 1],
            send_sem=mix_ssem.at[m - 1],
            recv_sem=mix_rsem.at[m - 1],
            device_id=(me, peer),
            device_id_type=MESH,
        )
        copy.start()
        mix_copies.append(copy)

    for p in range(pairs):
        k_parts = [None] * (blocks + 2)
        v_parts = [None] * (blocks + 2)
        k_coarse = v_coarse = None
        for n in range(blocks):
            u = p * blocks + n
            rows, cols = pl.ds(n * BLOCK, BLOCK), pl.ds(p * PAIR, PAIR)
            kf, kc = keys(p, n, 0)
            vf, vc = keys(p, n, 1)
            qs, gs = qstack[u], gstack[u]
            pf = weights[u, pl.ds(0, window), :]
            pc = weights[u, pl.ds(window, plan.coarse_rows), :]
            dl = delta[u]
            df = (pf.astype(F32) * (dot_nt(vf, gs) - dl)).astype(BF16)
            dc = (pc.astype(F32) * (dot_nt(vc, gs) - dl)).astype(BF16)
            dvf, dvc = dot_nn(pf, gs), dot_nn(pc, gs)
            dkf, dkc = dot_nn(df, qs), dot_nn(dc, qs)
            dq = heads_of(dot_tn(kf, df) + dot_tn(kc, dc)) * scale
            qg_ref[rows, cols] = dq.T.astype(BF16)
            for i in range(3):
                piece = slice(i * BLOCK, (i + 1) * BLOCK)
                old = k_parts[n + i]
                k_parts[n + i] = dkf[piece] if old is None else old + dkf[piece]
                old = v_parts[n + i]
                v_parts[n + i] = dvf[piece] if old is None else old + dvf[piece]
            k_coarse = dkc if k_coarse is None else k_coarse + dkc
            v_coarse = dvc if v_coarse is None else v_coarse + dvc
        for side, fine, far in ((0, k_parts, k_coarse), (1, v_parts, v_coarse)):
            cols = pl.ds(side * feats + p * PAIR, PAIR)
            rim_send[0, :, cols] = fine[0].astype(BF16)
            rim_send[1, :, cols] = fine[-1].astype(BF16)
            for n in range(blocks):
                inner[pl.ds(n * BLOCK, BLOCK), cols] = fine[n + 1]
            far = far.astype(BF16)
            grad[pl.ds(0, POOL_ROWS), cols] = far[:POOL_ROWS]
            for b in range(bits):
                level = far[POOL_ROWS * (1 + b) : POOL_ROWS * (2 + b)]
                if not plan.direct[b]:
                    level = dot_tn(compact_matrix(plan, b), level).astype(BF16)
                at = plan.grad_at[b] - POOL_ROWS
                cg_send[pl.ds(at, plan.slot[b] << b), cols] = level

    cg_copies = {}
    for m in reversed(range(1, n_seq)):
        b = m.bit_length() - 1
        at = plan.grad_at[b] + (m - (1 << b)) * plan.slot[b]
        copy = pltpu.make_async_remote_copy(
            src_ref=cg_send.at[pl.ds(at - POOL_ROWS, plan.slot[b]), :],
            dst_ref=grad.at[pl.ds(at, plan.slot[b]), :],
            send_sem=cg_ssem.at[m - 1],
            recv_sem=cg_rsem.at[m - 1],
            device_id=(flip(me, m), hme),
            device_id_type=MESH,
        )
        copy.start()
        cg_copies[m] = copy

    def rim(side):
        return pltpu.make_async_remote_copy(
            src_ref=rim_send.at[side],
            dst_ref=rim_recv.at[1 - side],
            send_sem=rim_ssem.at[side],
            recv_sem=rim_rsem.at[side],
            device_id=(me - 1 if side == 0 else me + 1, hme),
            device_id_type=MESH,
        )

    @pl.when(me > 0)
    def _():
        rim(0).start()

    @pl.when(me < n_seq - 1)
    def _():
        rim(1).start()

    even = ["own"] + list(range(0, bits, 2))
    odd = list(range(1, bits, 2))
    even_t = spread_matrix(plan, frames, even, 0, plan.even_rows)
    if odd:
        odd_t = spread_matrix(
            plan, frames, odd, plan.even_rows, plan.grad_rows - plan.even_rows
        )

    for copy in mix_copies:
        copy.wait()
    acc = mix_send[hme].astype(F32)
    for m in range(1, n_head):
        acc = acc + mix_recv[m - 1].astype(F32)
    mixed_ref[...] = acc.astype(BF16)

    for m in range(1, n_seq):
        cg_copies[m].wait()
    root = 1.0 / math.sqrt(plan.span)
    total = inner[...] + dot_nn(even_t, grad[pl.ds(0, plan.even_rows), :]) * root
    if odd:
        total = total + dot_nn(
            odd_t, grad[pl.ds(plan.even_rows, plan.grad_rows - plan.even_rows), :]
        ) * (root / math.sqrt(2.0))
    inner[...] = total

    @pl.when(me > 0)
    def _():
        rim(1).wait_recv()
        rim(0).wait_send()

    @pl.when(me < n_seq - 1)
    def _():
        rim(0).wait_recv()
        rim(1).wait_send()

    head_rows, tail_rows = pl.ds(0, BLOCK), pl.ds(frames - BLOCK, BLOCK)
    inner[head_rows, :] = inner[head_rows, :] + rim_recv[0].astype(F32)
    inner[tail_rows, :] = inner[tail_rows, :] + rim_recv[1].astype(F32)
    kg_ref[...] = inner[:, :feats].astype(BF16)
    vg_ref[...] = inner[:, feats:].astype(BF16)


def body(queries, key_rows, value_rows, out_weight, cotangent):
    frames, feats = queries.shape
    width = out_weight.shape[1]
    n_seq, n_head = lax.axis_size("seq"), lax.axis_size("head")
    plan = Plan(n_seq, frames)
    units = (frames // BLOCK) * (feats // PAIR)
    keys = 3 * BLOCK + plan.coarse_rows
    share = frames // n_head
    dma = pltpu.SemaphoreType.DMA
    return pl.pallas_call(
        functools.partial(kernel, n_seq, n_head, plan),
        out_shape=(
            jax.ShapeDtypeStruct((share, width), BF16),
            jax.ShapeDtypeStruct((frames, feats), BF16),
            jax.ShapeDtypeStruct((frames, feats), BF16),
            jax.ShapeDtypeStruct((frames, feats), BF16),
        ),
        in_specs=[pl.BlockSpec(memory_space=pl.ANY)] * 5,
        out_specs=tuple([pl.BlockSpec(memory_space=pltpu.VMEM)] * 4),
        scratch_shapes=[
            pltpu.VMEM((frames, feats), BF16),
            pltpu.VMEM((frames + 2 * BLOCK, 2 * feats), BF16),
            pltpu.VMEM((feats, width), BF16),
            pltpu.VMEM((frames, width), BF16),
            pltpu.VMEM((plan.send_rows, 2 * feats), BF16),
            pltpu.VMEM((plan.coarse_rows, 2 * feats), BF16),
            pltpu.VMEM((plan.wide_rows, 2 * feats), BF16),
            pltpu.VMEM((frames, feats), BF16),
            pltpu.VMEM((frames, feats), BF16),
            pltpu.VMEM((units, 2 * BLOCK, PAIR), BF16),
            pltpu.VMEM((units, 2 * BLOCK, PAIR), BF16),
            pltpu.VMEM((units, keys, 2 * BLOCK), BF16),
            pltpu.VMEM((units, 1, 2 * BLOCK), F32),
            pltpu.VMEM((n_head, share, width), BF16),
            pltpu.VMEM((max(n_head - 1, 1), share, width), BF16),
            pltpu.VMEM((2, BLOCK, 2 * feats), BF16),
            pltpu.VMEM((2, BLOCK, 2 * feats), BF16),
            pltpu.VMEM((frames, 2 * feats), F32),
            pltpu.VMEM((plan.grad_rows - POOL_ROWS, 2 * feats), BF16),
            pltpu.VMEM((plan.grad_rows, 2 * feats), BF16),
            dma((5,)),
            dma((2,)),
            dma((2,)),
            dma((n_seq - 1,)),
            dma((n_seq - 1,)),
            dma((2,)),
            dma((2,)),
            dma((n_seq - 1,)),
            dma((n_seq - 1,)),
            dma((n_head - 1,)),
            dma((n_head - 1,)),
        ],
        compiler_params=pltpu.CompilerParams(
            collective_id=0, has_side_effects=True, vmem_limit_bytes=32 * 1024 * 1024
        ),
    )(queries, key_rows, value_rows, out_weight, cotangent)


def solution(mesh):
    placed = (P("seq", "head"), P("seq", "head"), P("seq", "head"), P("head", None), P("seq", None))
    return jax.shard_map(
        body,
        mesh=mesh,
        in_specs=placed,
        out_specs=(P(("seq", "head"), None), P("seq", "head"), P("seq", "head"), P("seq", "head")),
        check_vma=False,
    )
```

time: 82.4 us -> 36.1 us (0.44)
  Pallas kernels: 0 us -> 27.7 us
  starting transfers between devices: 27.7 us -> 0 us
  between operations: 14.8 us -> 0.65 us
  matrix products: 12.4 us -> 0 us
  waiting for transfers between devices: 11.3 us -> 0 us
  local copies, waits for them, and re-layouts: 11.7 us -> 7.41 us
  other arithmetic: 4.09 us -> 0 us
    pallas_call x0 -> x1, Pallas kernels: none -> 27.7 us  [body(): pl.pallas_call(functools.partial(kernel, n_seq, n_head, plan), out_shape=...]
    ppermute x10 -> x0, starting transfers between devices: 27.7 us -> none  [the longest x6 15.5 us: from_partner(): return lax.ppermute(block, axis, route)]
    dot_general x14 -> x0, matrix products: 12.4 us -> none  [the longest x3 3.82 us: attend(): jnp.einsum('nhqk,nkhd->nqhd', fine_weights, fine_values, preferred_elemen...]
    ppermute x10 -> x0, waiting for transfers between devices: 11.3 us -> none  [the longest x6 8.48 us: from_partner(): return lax.ppermute(block, axis, route)]
    unnamed x38 -> x14, local copies, waits for them, and re-layouts: 2.75 us -> 7.41 us
    slice x15 -> x0, local copies, waits for them, and re-layouts: 4.65 us -> none  [the longest x2 1.43 us: attend(): coarse_tiles[:, feature_width:].reshape(-1, head_count, HEAD_DIM)]
    convert_element_type x5 -> x0, other arithmetic: 1.22 us -> none  [the longest x1 1.12 us: attend(): window_block.astype(jnp.bfloat16)]
    reshape x11 -> x0, local copies, waits for them, and re-layouts: 1.1 us -> none  [the longest x4 0.29 us: pair_pool(): panel.reshape(panel.shape[:-2] + (row_count // 2, 2, panel.shape[-1]))]
  transfers between devices with their start and end apart: 11 -> 0, of which waited for: 6 -> 0; matrix products, arithmetic and copies ran while one was open for 11% -> 0% of each run, Pallas kernels for 0% -> 0%
where the time goes in v1:
time: 36.1 us; the launch traced here: 35.8 us
  Pallas kernels  27.7 us (77%)
  local copies, waits for them, and re-layouts  7.41 us (21%)
  between operations  0.65 us (2%)
    pallas_call x1, Pallas kernels, body(): pl.pallas_call(functools.partial(kernel, n_seq, n_head, plan), out_shape=...  27.7 us
    unnamed x14, local copies, waits for them, and re-layouts  7.41 us

profile of v1, /device:TPU:0, one launch (start us, length us, event | category | flops | bytes accessed | tf_op | source)
XLA Modules:
  0.0 35.8 jit_solution(18093009560357918878)
XLA Ops:
  0.6 0.0 copy-start
  0.6 1.0 %copy-done = bf16[256,1024]{1,0:T(8,128)(2,1)S(1)} copy-done((bf16[256,1024]{1,0:T(8,128)(2,1)S(1)}, bf16[256,1024]{1,0:T(8,128)(2,1)}, u32[]{:S(2)}) %copy-start) | copy-done | bytes 524312
  1.7 0.0 copy-start.1
  1.7 1.0 %copy-done.1 = bf16[256,1024]{1,0:T(8,128)(2,1)S(1)} copy-done((bf16[256,1024]{1,0:T(8,128)(2,1)S(1)}, bf16[256,1024]{1,0:T(8,128)(2,1)}, u32[]{:S(2)}) %copy-start.1) | copy-done | bytes 524312
  2.7 0.0 copy-start.2
  2.7 0.9 %copy-done.2 = bf16[256,256]{1,0:T(8,128)(2,1)S(1)} copy-done((bf16[256,256]{1,0:T(8,128)(2,1)S(1)}, bf16[256,256]{1,0:T(8,128)(2,1)}, u32[]{:S(2)}) %copy-start.2) | copy-done | bytes 131096
  3.6 0.0 copy-start.3
  3.6 0.9 %copy-done.3 = bf16[256,256]{1,0:T(8,128)(2,1)S(1)} copy-done((bf16[256,256]{1,0:T(8,128)(2,1)S(1)}, bf16[256,256]{1,0:T(8,128)(2,1)}, u32[]{:S(2)}) %copy-start.3) | copy-done | bytes 131096
  4.5 0.0 copy-start.4
  4.5 0.9 %copy-done.4 = bf16[256,256]{1,0:T(8,128)(2,1)S(1)} copy-done((bf16[256,256]{1,0:T(8,128)(2,1)S(1)}, bf16[256,256]{1,0:T(8,128)(2,1)}, u32[]{:S(2)}) %copy-start.4) | copy-done | bytes 131096
  5.4 27.7 %shard_map.84 = (bf16[64,1024]{1,0:T(8,128)(2,1)S(1)}, bf16[256,256]{1,0:T(8,128)(2,1)S(1)}, bf16[256,256]{1,0:T(8,128)(2,1)S(1)}, bf16[256,256]{1,0:T(8,128)(2,1)S(1)}) custom-call(bf16[256,256]{1,0:T(8,128)(2,1)S(1)} %copy-done.2, bf16[256,256]{1,0:T(8,128)(2,1)S(1)} %copy-done.3, bf16[256,256]{1,0:T(8,128)(2,1)S(1)} %copy-done.4, ...), custom_call_target="tpu_custom_call" | custom-call | tf_op jit(solution)/shard_map/pallas_call | solution.py:476
  33.2 0.7 %copy.13 = bf16[64,1024]{1,0:T(8,128)(2,1)} copy(bf16[64,1024]{1,0:T(8,128)(2,1)S(1)} %get-tuple-element.8) | data formatting | bytes 262144
  33.8 0.7 %copy.14 = bf16[256,256]{1,0:T(8,128)(2,1)} copy(bf16[256,256]{1,0:T(8,128)(2,1)S(1)} %get-tuple-element.9) | data formatting | bytes 262144
  34.5 0.7 %copy.15 = bf16[256,256]{1,0:T(8,128)(2,1)} copy(bf16[256,256]{1,0:T(8,128)(2,1)S(1)} %get-tuple-element.10) | data formatting | bytes 262144
  35.2 0.7 %copy.16 = bf16[256,256]{1,0:T(8,128)(2,1)} copy(bf16[256,256]{1,0:T(8,128)(2,1)S(1)} %get-tuple-element.11) | data formatting | bytes 262144
Async XLA Ops:
  0.6 1.0 %copy-start = (bf16[256,1024]{1,0:T(8,128)(2,1)S(1)}, bf16[256,1024]{1,0:T(8,128)(2,1)}, u32[]{:S(2)}) copy-start(bf16[256,1024]{1,0:T(8,128)(2,1)} %w_hbm.1) | copy-start | bytes 1572868
  1.7 1.0 %copy-start.1 = (bf16[256,1024]{1,0:T(8,128)(2,1)S(1)}, bf16[256,1024]{1,0:T(8,128)(2,1)}, u32[]{:S(2)}) copy-start(bf16[256,1024]{1,0:T(8,128)(2,1)} %c_hbm.1) | copy-start | bytes 1572868
  2.7 0.9 %copy-start.2 = (bf16[256,256]{1,0:T(8,128)(2,1)S(1)}, bf16[256,256]{1,0:T(8,128)(2,1)}, u32[]{:S(2)}) copy-start(bf16[256,256]{1,0:T(8,128)(2,1)} %q_hbm.1) | copy-start | bytes 393220
  3.6 0.9 %copy-start.3 = (bf16[256,256]{1,0:T(8,128)(2,1)S(1)}, bf16[256,256]{1,0:T(8,128)(2,1)}, u32[]{:S(2)}) copy-start(bf16[256,256]{1,0:T(8,128)(2,1)} %k_hbm.1) | copy-start | bytes 393220
  4.5 0.9 %copy-start.4 = (bf16[256,256]{1,0:T(8,128)(2,1)S(1)}, bf16[256,256]{1,0:T(8,128)(2,1)}, u32[]{:S(2)}) copy-start(bf16[256,256]{1,0:T(8,128)(2,1)} %v_hbm.1) | copy-start | bytes 393220

commit v2 on v1

--- a/solution.py
+++ b/solution.py
@@ -464,6 +464,15 @@
     vg_ref[...] = inner[:, feats:].astype(BF16)
 
 
+def put_out(a0, a1, a2, a3, b0, b1, b2, b3, sem):
+    pairs = zip((a0, a1, a2, a3), (b0, b1, b2, b3))
+    copies = [pltpu.make_async_copy(a, b, sem.at[i]) for i, (a, b) in enumerate(pairs)]
+    for copy in copies:
+        copy.start()
+    for copy in copies:
+        copy.wait()
+
+
 def body(queries, key_rows, value_rows, out_weight, cotangent):
     frames, feats = queries.shape
     width = out_weight.shape[1]
@@ -473,15 +482,17 @@
     keys = 3 * BLOCK + plan.coarse_rows
     share = frames // n_head
     dma = pltpu.SemaphoreType.DMA
-    return pl.pallas_call(
+    operands = (queries, key_rows, value_rows, out_weight, cotangent)
+    shapes = (
+        jax.ShapeDtypeStruct((share, width), BF16),
+        jax.ShapeDtypeStruct((frames, feats), BF16),
+        jax.ShapeDtypeStruct((frames, feats), BF16),
+        jax.ShapeDtypeStruct((frames, feats), BF16),
+    )
+    results = pl.pallas_call(
         functools.partial(kernel, n_seq, n_head, plan),
-        out_shape=(
-            jax.ShapeDtypeStruct((share, width), BF16),
-            jax.ShapeDtypeStruct((frames, feats), BF16),
-            jax.ShapeDtypeStruct((frames, feats), BF16),
-            jax.ShapeDtypeStruct((frames, feats), BF16),
-        ),
-        in_specs=[pl.BlockSpec(memory_space=pl.ANY)] * 5,
+        out_shape=shapes,
+        in_specs=[pl.BlockSpec(memory_space=pltpu.HBM)] * 5,
         out_specs=tuple([pl.BlockSpec(memory_space=pltpu.VMEM)] * 4),
         scratch_shapes=[
             pltpu.VMEM((frames, feats), BF16),
@@ -519,7 +530,15 @@
         compiler_params=pltpu.CompilerParams(
             collective_id=0, has_side_effects=True, vmem_limit_bytes=32 * 1024 * 1024
         ),
-    )(queries, key_rows, value_rows, out_weight, cotangent)
+    )(*[pltpu.with_memory_space_constraint(x, pltpu.HBM) for x in operands])
+    return pl.pallas_call(
+        put_out,
+        out_shape=shapes,
+        in_specs=[pl.BlockSpec(memory_space=pl.ANY)] * 4,
+        out_specs=tuple([pl.BlockSpec(memory_space=pltpu.HBM)] * 4),
+        scratch_shapes=[dma((4,))],
+        compiler_params=pltpu.CompilerParams(vmem_limit_bytes=1024 * 1024),
+    )(*results)
 
 
 def solution(mesh):

time: 36.1 us -> 29.1 us (0.81)
  local copies, waits for them, and re-layouts: 7.41 us -> 0 us
  Pallas kernels: 27.7 us -> 28.3 us
    unnamed x14 -> x0, local copies, waits for them, and re-layouts: 7.41 us -> none
    pallas_call x0 -> x1, Pallas kernels: none -> 0.82 us  [body(): pl.pallas_call(put_out, out_shape=shapes, in_specs=[pl.BlockSpec(memory_s...]
where the time goes in v2:
time: 29.1 us; the launch traced here: 29 us
  Pallas kernels  28.3 us (97%)
  between operations  0.64 us (2%)
    pallas_call x1, Pallas kernels, body(): pl.pallas_call(functools.partial(kernel, n_seq, n_head, plan), out_shape=...  27.5 us
    pallas_call x1, Pallas kernels, body(): pl.pallas_call(put_out, out_shape=shapes, in_specs=[pl.BlockSpec(memory_s...  0.82 us

profile of v2, /device:TPU:0, one launch (start us, length us, event | category | flops | bytes accessed | tf_op | source)
XLA Modules:
  0.0 29.0 jit_solution(16765953302002454224)
XLA Ops:
  0.6 27.5 %shard_map.84 = (bf16[64,1024]{1,0:T(8,128)(2,1)S(1)}, bf16[256,256]{1,0:T(8,128)(2,1)S(1)}, bf16[256,256]{1,0:T(8,128)(2,1)S(1)}, bf16[256,256]{1,0:T(8,128)(2,1)S(1)}) custom-call(bf16[256,256]{1,0:T(8,128)(2,1)} %q_hbm.1, bf16[256,256]{1,0:T(8,128)(2,1)} %k_hbm.1, bf16[256,256]{1,0:T(8,128)(2,1)} %v_hbm.1, bf16[256,1024]{1,0:T(8,128)(2,1)} %w_hbm.1, ...), custom_call_target="tpu_custom_call" | custom-call | tf_op jit(solution)/shard_map/pallas_call | solution.py:492
  28.2 0.8 %shard_map.85 = (bf16[64,1024]{1,0:T(8,128)(2,1)}, bf16[256,256]{1,0:T(8,128)(2,1)}, bf16[256,256]{1,0:T(8,128)(2,1)}, bf16[256,256]{1,0:T(8,128)(2,1)}) custom-call(bf16[64,1024]{1,0:T(8,128)(2,1)S(1)} %get-tuple-element.8.a0, bf16[256,256]{1,0:T(8,128)(2,1)S(1)} %get-tuple-element.9.a1, bf16[256,256]{1,0:T(8,128)(2,1)S(1)} %get-tuple-element.10.a2, ...), custom_call_target="tpu_custom_call" | custom-call | tf_op jit(solution)/shard_map/pallas_call | solution.py:534

commit v3 on v2

v3 whole, which is shorter than its diff:
```python
import functools
import math

import jax
import jax.numpy as jnp
from jax import lax
from jax.experimental import pallas as pl
from jax.experimental.pallas import tpu as pltpu
from jax.sharding import PartitionSpec as P

HEAD_DIM = 64
PAIR = 2 * HEAD_DIM
BLOCK = 128
POOL_ROWS = 64
MIN_SLOT = 16
MASKED = -1000000000.0
MESH = pl.DeviceIdType.MESH
F32 = jnp.float32
BF16 = jnp.bfloat16


def dot_nn(a, b):
    return lax.dot_general(a, b, (((1,), (0,)), ((), ())), preferred_element_type=F32)


def dot_nt(a, b):
    return lax.dot_general(a, b, (((1,), (1,)), ((), ())), preferred_element_type=F32)


def dot_tn(a, b):
    return lax.dot_general(a, b, (((0,), (0,)), ((), ())), preferred_element_type=F32)


class Plan:
    def __init__(self, n_seq, frames):
        self.bits = n_seq.bit_length() - 1
        self.span = frames // POOL_ROWS
        self.rows = [POOL_ROWS >> b for b in range(self.bits)]
        self.slot = [max(MIN_SLOT, r) for r in self.rows]
        self.send_at, at = [], 0
        for b in range(self.bits):
            self.send_at.append(at)
            at += self.slot[b]
        self.send_rows = at
        self.coarse_rows = POOL_ROWS * (1 + self.bits)
        self.direct = [r >= MIN_SLOT for r in self.rows]
        self.wide_at, at = {}, 0
        for b in range(self.bits):
            if not self.direct[b]:
                self.wide_at[b] = at
                at += self.slot[b] << b
        self.wide_rows = max(at, MIN_SLOT)
        self.grad_at, at = {"own": 0}, POOL_ROWS
        for b in range(0, self.bits, 2):
            self.grad_at[b] = at
            at += self.slot[b] << b
        self.even_rows = at
        for b in range(1, self.bits, 2):
            self.grad_at[b] = at
            at += self.slot[b] << b
        self.grad_rows = at


def flip(me, m):
    out, b = me, 0
    while m >> b:
        if (m >> b) & 1:
            out = out + (1 << b) * (1 - 2 * (me // (1 << b) % 2))
        b += 1
    return out


def pool_matrix(plan, frames):
    row = lax.broadcasted_iota(jnp.int32, (plan.send_rows, frames), 0)
    col = lax.broadcasted_iota(jnp.int32, (plan.send_rows, frames), 1)
    hit = None
    for b in range(plan.bits):
        width = plan.span << b
        lo = plan.send_at[b]
        rel = col - (row - lo) * width
        now = (row >= lo) & (row < lo + plan.slot[b]) & (rel >= 0) & (rel < width)
        hit = now if hit is None else hit | now
    return jnp.where(hit, 1.0, 0.0).astype(BF16)


def spread_matrix(plan, frames, levels, base, width_all):
    frame = lax.broadcasted_iota(jnp.int32, (frames, width_all), 0)
    col = lax.broadcasted_iota(jnp.int32, (frames, width_all), 1)
    out = jnp.zeros((frames, width_all), F32)
    for level in levels:
        b = 0 if level == "own" else level
        lo = plan.grad_at[level] - base
        total = POOL_ROWS if level == "own" else plan.slot[b] << b
        width = plan.span << b
        rel = frame - ((col - lo) & (plan.slot[b] - 1)) * width
        hit = (col >= lo) & (col < lo + total) & (rel >= 0) & (rel < width)
        out = jnp.where(hit, 0.5 ** (b // 2), out)
    return out.astype(BF16)


def compact_matrix(plan, b):
    total = plan.slot[b] << b
    row = lax.broadcasted_iota(jnp.int32, (POOL_ROWS, total), 0)
    col = lax.broadcasted_iota(jnp.int32, (POOL_ROWS, total), 1)
    r = plan.rows[b]
    hit = ((col // plan.slot[b]) == (row // r)) & ((col & (plan.slot[b] - 1)) == (row & (r - 1)))
    return jnp.where(hit, 1.0, 0.0).astype(BF16)


def kernel(
    n_seq,
    n_head,
    plan,
    q_hbm,
    k_hbm,
    v_hbm,
    w_hbm,
    c_hbm,
    mixed_ref,
    qg_ref,
    kg_ref,
    vg_ref,
    q_ref,
    ext,
    w_ref,
    c_ref,
    pool_send,
    coarse,
    wide,
    hgrad,
    heads,
    qstack,
    gstack,
    weights,
    delta,
    mix_send,
    mix_recv,
    rim_send,
    rim_recv,
    inner,
    cg_send,
    grad,
    spread,
    load_sem,
    halo_ssem,
    halo_rsem,
    pool_ssem,
    pool_rsem,
    rim_ssem,
    rim_rsem,
    cg_ssem,
    cg_rsem,
    mix_ssem,
    mix_rsem,
):
    me = lax.axis_index("seq")
    hme = lax.axis_index("head")
    frames, feats = q_ref.shape
    blocks = frames // BLOCK
    pairs = feats // PAIR
    bits = plan.bits
    window = 3 * BLOCK
    peers = n_seq - 1

    own_rows = pl.ds(BLOCK, frames)
    k_cols, v_cols = pl.ds(0, PAIR), pl.ds(PAIR, PAIR)
    loads = []
    for p in range(pairs):
        cols = pl.ds(p * PAIR, PAIR)
        for side, (hbm, to) in enumerate(((k_hbm, k_cols), (v_hbm, v_cols))):
            loads.append(
                pltpu.make_async_copy(
                    hbm.at[:, cols], ext.at[p, own_rows, to], load_sem.at[2 * p + side]
                )
            )
    for i, (hbm, ref) in enumerate(((c_hbm, c_ref), (w_hbm, w_ref), (q_hbm, q_ref))):
        loads.append(pltpu.make_async_copy(hbm, ref, load_sem.at[2 * pairs + i]))
    for load in loads:
        load.start()

    barrier = pltpu.get_barrier_semaphore()
    for m in reversed(range(1, n_seq)):
        pl.semaphore_signal(barrier, inc=1, device_id=(flip(me, m), hme), device_id_type=MESH)
    for m in range(1, n_head):
        pl.semaphore_signal(
            barrier, inc=1, device_id=(me, lax.rem(hme + m, n_head)), device_id_type=MESH
        )

    @pl.when(me == 0)
    def _():
        for p in range(pairs):
            ext[p, pl.ds(0, BLOCK), :] = jnp.zeros((BLOCK, 2 * PAIR), BF16)
            rim_recv[p, 0] = jnp.zeros((BLOCK, 2 * PAIR), BF16)

    @pl.when(me == n_seq - 1)
    def _():
        for p in range(pairs):
            ext[p, pl.ds(BLOCK + frames, BLOCK), :] = jnp.zeros((BLOCK, 2 * PAIR), BF16)
            rim_recv[p, 1] = jnp.zeros((BLOCK, 2 * PAIR), BF16)

    pooling = pool_matrix(plan, frames)
    for p in range(pairs):
        loads[2 * p].wait()
        loads[2 * p + 1].wait()
        sums = dot_nn(pooling, ext[p, own_rows, :])
        for b in range(bits):
            at = plan.send_at[b]
            level = sums[at : at + plan.slot[b]] * (1.0 / math.sqrt(plan.span << b))
            pool_send[p, pl.ds(at, plan.slot[b]), :] = level.astype(BF16)
            if b == 0:
                coarse[p, pl.ds(0, POOL_ROWS), :] = level.astype(BF16)

    def halo(p, side):
        return pltpu.make_async_remote_copy(
            src_ref=ext.at[p, pl.ds(frames if side == 0 else BLOCK, BLOCK), :],
            dst_ref=ext.at[p, pl.ds(0 if side == 0 else BLOCK + frames, BLOCK), :],
            send_sem=halo_ssem.at[2 * p + side],
            recv_sem=halo_rsem.at[2 * p + side],
            device_id=(me + 1 if side == 0 else me - 1, hme),
            device_id_type=MESH,
        )

    def panel(p, m):
        b = m.bit_length() - 1
        slot = m - (1 << b)
        if plan.direct[b]:
            at = POOL_ROWS * (1 + b) + slot * plan.slot[b]
            landing = coarse.at[p, pl.ds(at, plan.slot[b]), :]
        else:
            at = plan.wide_at[b] + slot * plan.slot[b]
            landing = wide.at[p, pl.ds(at, plan.slot[b]), :]
        return pltpu.make_async_remote_copy(
            src_ref=pool_send.at[p, pl.ds(plan.send_at[b], plan.slot[b]), :],
            dst_ref=landing,
            send_sem=pool_ssem.at[p * peers + m - 1],
            recv_sem=pool_rsem.at[p * peers + m - 1],
            device_id=(flip(me, m), hme),
            device_id_type=MESH,
        )

    def far_grad(p, m):
        b = m.bit_length() - 1
        at = plan.grad_at[b] + (m - (1 << b)) * plan.slot[b]
        return pltpu.make_async_remote_copy(
            src_ref=cg_send.at[p, pl.ds(at - POOL_ROWS, plan.slot[b]), :],
            dst_ref=grad.at[p, pl.ds(at, plan.slot[b]), :],
            send_sem=cg_ssem.at[p * peers + m - 1],
            recv_sem=cg_rsem.at[p * peers + m - 1],
            device_id=(flip(me, m), hme),
            device_id_type=MESH,
        )

    def rim(p, side):
        return pltpu.make_async_remote_copy(
            src_ref=rim_send.at[p, side],
            dst_ref=rim_recv.at[p, 1 - side],
            send_sem=rim_ssem.at[2 * p + side],
            recv_sem=rim_rsem.at[2 * p + side],
            device_id=(me - 1 if side == 0 else me + 1, hme),
            device_id_type=MESH,
        )

    pl.semaphore_wait(barrier, n_seq - 1 + n_head - 1)

    for p in range(pairs):
        for m in reversed(range(1, n_seq)):
            panel(p, m).start()

        @pl.when(me < n_seq - 1)
        def _():
            halo(p, 0).start()

        @pl.when(me > 0)
        def _():
            halo(p, 1).start()

    for load in loads[2 * pairs :]:
        load.wait()
    hgrad[...] = dot_nt(c_ref[...], w_ref[...]).astype(BF16)

    lane = lax.broadcasted_iota(jnp.int32, (BLOCK, PAIR), 1)
    first = lane < HEAD_DIM

    def stacked(block):
        zero = jnp.zeros_like(block)
        return jnp.concatenate(
            [jnp.where(first, block, zero), jnp.where(first, zero, block)], axis=0
        )

    scale = 1.0 / math.sqrt(HEAD_DIM)
    for p in range(pairs):
        for n in range(blocks):
            u = p * blocks + n
            rows, cols = pl.ds(n * BLOCK, BLOCK), pl.ds(p * PAIR, PAIR)
            qstack[u] = (stacked(q_ref[rows, cols].astype(F32)) * scale).astype(BF16)
            gstack[u] = stacked(hgrad[rows, cols].astype(F32)).astype(BF16)

    even = ["own"] + list(range(0, bits, 2))
    odd = list(range(1, bits, 2))
    spread[:, pl.ds(0, plan.even_rows)] = spread_matrix(plan, frames, even, 0, plan.even_rows)
    odd_rows = plan.grad_rows - plan.even_rows
    if odd:
        spread[:, pl.ds(plan.even_rows, odd_rows)] = spread_matrix(
            plan, frames, odd, plan.even_rows, odd_rows
        )

    left_bias = jnp.where(me == 0, MASKED, 0.0).astype(F32)
    right_bias = jnp.where(me == n_seq - 1, MASKED, 0.0).astype(F32)

    def keys(p, n, cols):
        return ext[p, pl.ds(n * BLOCK, window), cols], coarse[p, :, cols]

    def heads_of(both):
        return jnp.concatenate([both[:HEAD_DIM, :BLOCK], both[HEAD_DIM:, BLOCK:]], axis=0)

    def arrive(p):
        for m in range(1, n_seq):
            panel(p, m).wait()

        @pl.when(me > 0)
        def _():
            halo(p, 0).wait_recv()
            halo(p, 1).wait_send()

        @pl.when(me < n_seq - 1)
        def _():
            halo(p, 1).wait_recv()
            halo(p, 0).wait_send()

        for b in range(bits):
            if not plan.direct[b]:
                packed = wide[p, pl.ds(plan.wide_at[b], plan.slot[b] << b), :]
                coarse[p, pl.ds(POOL_ROWS * (1 + b), POOL_ROWS), :] = dot_nn(
                    compact_matrix(plan, b), packed
                ).astype(BF16)

    def forward(p):
        for n in range(blocks):
            u = p * blocks + n
            rows, cols = pl.ds(n * BLOCK, BLOCK), pl.ds(p * PAIR, PAIR)
            kf, kc = keys(p, n, k_cols)
            vf, vc = keys(p, n, v_cols)
            qs = qstack[u]
            sf = dot_nt(kf, qs)
            sc = dot_nt(kc, qs)
            parts = [sf[i * BLOCK : (i + 1) * BLOCK] for i in range(3)]
            if n == 0:
                parts[0] = parts[0] + left_bias
            if n == blocks - 1:
                parts[2] = parts[2] + right_bias
            parts.append(sc)
            top = functools.reduce(jnp.maximum, [x.max(axis=0, keepdims=True) for x in parts])
            parts = [jnp.exp(x - top) for x in parts]
            total = sum(x.sum(axis=0, keepdims=True) for x in parts)
            inv = 1.0 / total
            parts = [(x * inv).astype(BF16) for x in parts]
            pf = jnp.concatenate(parts[:3], axis=0)
            pc = parts[3]
            weights[u, pl.ds(0, window), :] = pf
            weights[u, pl.ds(window, plan.coarse_rows), :] = pc
            out = heads_of(dot_tn(vf, pf) + dot_tn(vc, pc))
            heads[rows, cols] = out.T.astype(BF16)
            prod = out * hgrad[rows, cols].astype(F32).T
            delta[u] = jnp.concatenate(
                [
                    prod[:HEAD_DIM].sum(axis=0, keepdims=True),
                    prod[HEAD_DIM:].sum(axis=0, keepdims=True),
                ],
                axis=1,
            )

    def backward(p):
        k_parts = [None] * (blocks + 2)
        v_parts = [None] * (blocks + 2)
        k_coarse = v_coarse = None
        for n in range(blocks):
            u = p * blocks + n
            rows, cols = pl.ds(n * BLOCK, BLOCK), pl.ds(p * PAIR, PAIR)
            kf, kc = keys(p, n, k_cols)
            vf, vc = keys(p, n, v_cols)
            qs, gs = qstack[u], gstack[u]
            pf = weights[u, pl.ds(0, window), :]
            pc = weights[u, pl.ds(window, plan.coarse_rows), :]
            dl = delta[u]
            df = (pf.astype(F32) * (dot_nt(vf, gs) - dl)).astype(BF16)
            dc = (pc.astype(F32) * (dot_nt(vc, gs) - dl)).astype(BF16)
            dvf, dvc = dot_nn(pf, gs), dot_nn(pc, gs)
            dkf, dkc = dot_nn(df, qs), dot_nn(dc, qs)
            dq = heads_of(dot_tn(kf, df) + dot_tn(kc, dc)) * scale
            qg_ref[rows, cols] = dq.T.astype(BF16)
            for i in range(3):
                piece = slice(i * BLOCK, (i + 1) * BLOCK)
                old = k_parts[n + i]
                k_parts[n + i] = dkf[piece] if old is None else old + dkf[piece]
                old = v_parts[n + i]
                v_parts[n + i] = dvf[piece] if old is None else old + dvf[piece]
            k_coarse = dkc if k_coarse is None else k_coarse + dkc
            v_coarse = dvc if v_coarse is None else v_coarse + dvc
        for fine, far, cols in ((k_parts, k_coarse, k_cols), (v_parts, v_coarse, v_cols)):
            rim_send[p, 0, :, cols] = fine[0].astype(BF16)
            rim_send[p, 1, :, cols] = fine[-1].astype(BF16)
            for n in range(blocks):
                inner[p, pl.ds(n * BLOCK, BLOCK), cols] = fine[n + 1]
            far = far.astype(BF16)
            grad[p, pl.ds(0, POOL_ROWS), cols] = far[:POOL_ROWS]
            for b in range(bits):
                level = far[POOL_ROWS * (1 + b) : POOL_ROWS * (2 + b)]
                if not plan.direct[b]:
                    level = dot_tn(compact_matrix(plan, b), level).astype(BF16)
                at = plan.grad_at[b] - POOL_ROWS
                cg_send[p, pl.ds(at, plan.slot[b] << b), cols] = level

        for m in reversed(range(1, n_seq)):
            far_grad(p, m).start()

        @pl.when(me > 0)
        def _():
            rim(p, 0).start()

        @pl.when(me < n_seq - 1)
        def _():
            rim(p, 1).start()

    share = frames // n_head

    def mix(m):
        peer = lax.rem(hme + m, n_head)
        return pltpu.make_async_remote_copy(
            src_ref=mix_send.at[peer],
            dst_ref=mix_recv.at[m - 1],
            send_sem=mix_ssem.at[m - 1],
            recv_sem=mix_rsem.at[m - 1],
            device_id=(me, peer),
            device_id_type=MESH,
        )

    for p in range(pairs):
        arrive(p)
        forward(p)
        if p == pairs - 1:
            mixed = dot_nn(heads[...], w_ref[...]).astype(BF16)
            for h in range(n_head):
                mix_send[h] = mixed[h * share : (h + 1) * share]
            for m in range(1, n_head):
                mix(m).start()
        backward(p)

    root = 1.0 / math.sqrt(plan.span)
    head_rows, tail_rows = pl.ds(0, BLOCK), pl.ds(frames - BLOCK, BLOCK)

    def collect(p):
        for m in range(1, n_seq):
            far_grad(p, m).wait()
        total = inner[p] + root * dot_nn(
            spread[:, pl.ds(0, plan.even_rows)], grad[p, pl.ds(0, plan.even_rows), :]
        )
        if odd:
            total = total + (root / math.sqrt(2.0)) * dot_nn(
                spread[:, pl.ds(plan.even_rows, odd_rows)],
                grad[p, pl.ds(plan.even_rows, odd_rows), :],
            )
        inner[p] = total

        @pl.when(me > 0)
        def _():
            rim(p, 1).wait_recv()
            rim(p, 0).wait_send()

        @pl.when(me < n_seq - 1)
        def _():
            rim(p, 0).wait_recv()
            rim(p, 1).wait_send()

        inner[p, head_rows, :] = inner[p, head_rows, :] + rim_recv[p, 0].astype(F32)
        inner[p, tail_rows, :] = inner[p, tail_rows, :] + rim_recv[p, 1].astype(F32)
        cols = pl.ds(p * PAIR, PAIR)
        kg_ref[:, cols] = inner[p, :, k_cols].astype(BF16)
        vg_ref[:, cols] = inner[p, :, v_cols].astype(BF16)

    for p in range(pairs - 1):
        collect(p)
    for m in range(1, n_head):
        mix(m).wait()
    acc = mix_send[hme].astype(F32)
    for m in range(1, n_head):
        acc = acc + mix_recv[m - 1].astype(F32)
    mixed_ref[...] = acc.astype(BF16)
    collect(pairs - 1)


def put_out(a0, a1, a2, a3, b0, b1, b2, b3, sem):
    pairs = zip((a0, a1, a2, a3), (b0, b1, b2, b3))
    copies = [pltpu.make_async_copy(a, b, sem.at[i]) for i, (a, b) in enumerate(pairs)]
    for copy in copies:
        copy.start()
    for copy in copies:
        copy.wait()


def body(queries, key_rows, value_rows, out_weight, cotangent):
    frames, feats = queries.shape
    width = out_weight.shape[1]
    n_seq, n_head = lax.axis_size("seq"), lax.axis_size("head")
    plan = Plan(n_seq, frames)
    pairs, wide = feats // PAIR, 2 * PAIR
    units = (frames // BLOCK) * pairs
    keys = 3 * BLOCK + plan.coarse_rows
    share = frames // n_head
    dma = pltpu.SemaphoreType.DMA
    operands = (queries, key_rows, value_rows, out_weight, cotangent)
    shapes = (
        jax.ShapeDtypeStruct((share, width), BF16),
        jax.ShapeDtypeStruct((frames, feats), BF16),
        jax.ShapeDtypeStruct((frames, feats), BF16),
        jax.ShapeDtypeStruct((frames, feats), BF16),
    )
    results = pl.pallas_call(
        functools.partial(kernel, n_seq, n_head, plan),
        out_shape=shapes,
        in_specs=[pl.BlockSpec(memory_space=pltpu.HBM)] * 5,
        out_specs=tuple([pl.BlockSpec(memory_space=pltpu.VMEM)] * 4),
        scratch_shapes=[
            pltpu.VMEM((frames, feats), BF16),
            pltpu.VMEM((pairs, frames + 2 * BLOCK, wide), BF16),
            pltpu.VMEM((feats, width), BF16),
            pltpu.VMEM((frames, width), BF16),
            pltpu.VMEM((pairs, plan.send_rows, wide), BF16),
            pltpu.VMEM((pairs, plan.coarse_rows, wide), BF16),
            pltpu.VMEM((pairs, plan.wide_rows, wide), BF16),
            pltpu.VMEM((frames, feats), BF16),
            pltpu.VMEM((frames, feats), BF16),
            pltpu.VMEM((units, 2 * BLOCK, PAIR), BF16),
            pltpu.VMEM((units, 2 * BLOCK, PAIR), BF16),
            pltpu.VMEM((units, keys, 2 * BLOCK), BF16),
            pltpu.VMEM((units, 1, 2 * BLOCK), F32),
            pltpu.VMEM((n_head, share, width), BF16),
            pltpu.VMEM((max(n_head - 1, 1), share, width), BF16),
            pltpu.VMEM((pairs, 2, BLOCK, wide), BF16),
            pltpu.VMEM((pairs, 2, BLOCK, wide), BF16),
            pltpu.VMEM((pairs, frames, wide), F32),
            pltpu.VMEM((pairs, plan.grad_rows - POOL_ROWS, wide), BF16),
            pltpu.VMEM((pairs, plan.grad_rows, wide), BF16),
            pltpu.VMEM((frames, plan.grad_rows), BF16),
            dma((2 * pairs + 3,)),
            dma((2 * pairs,)),
            dma((2 * pairs,)),
            dma((pairs * (n_seq - 1),)),
            dma((pairs * (n_seq - 1),)),
            dma((2 * pairs,)),
            dma((2 * pairs,)),
            dma((pairs * (n_seq - 1),)),
            dma((pairs * (n_seq - 1),)),
            dma((n_head - 1,)),
            dma((n_head - 1,)),
        ],
        compiler_params=pltpu.CompilerParams(
            collective_id=0, has_side_effects=True, vmem_limit_bytes=32 * 1024 * 1024
        ),
    )(*[pltpu.with_memory_space_constraint(x, pltpu.HBM) for x in operands])
    return pl.pallas_call(
        put_out,
        out_shape=shapes,
        in_specs=[pl.BlockSpec(memory_space=pl.ANY)] * 4,
        out_specs=tuple([pl.BlockSpec(memory_space=pltpu.HBM)] * 4),
        scratch_shapes=[dma((4,))],
        compiler_params=pltpu.CompilerParams(vmem_limit_bytes=1024 * 1024),
    )(*results)


def solution(mesh):
    placed = (P("seq", "head"), P("seq", "head"), P("seq", "head"), P("head", None), P("seq", None))
    return jax.shard_map(
        body,
        mesh=mesh,
        in_specs=placed,
        out_specs=(P(("seq", "head"), None), P("seq", "head"), P("seq", "head"), P("seq", "head")),
        check_vma=False,
    )
```

time: 29.1 us -> 26.8 us (0.921)
  the two profiles are of different devices: /device:TPU:0 before, /device:TPU:3 now
where the time goes in v3:
time: 26.8 us; the launch traced here: 26.7 us
  Pallas kernels  26 us (97%)
  between operations  0.64 us (2%)
    pallas_call x1, Pallas kernels, body(): pl.pallas_call(functools.partial(kernel, n_seq, n_head, plan), out_shape=...  25.2 us
    pallas_call x1, Pallas kernels, body(): pl.pallas_call(put_out, out_shape=shapes, in_specs=[pl.BlockSpec(memory_s...  0.82 us

profile of v3, /device:TPU:3, one launch (start us, length us, event | category | flops | bytes accessed | tf_op | source)
XLA Modules:
  0.0 26.7 jit_solution(14015558433047927072)
XLA Ops:
  0.6 25.2 %shard_map.84 = (bf16[64,1024]{1,0:T(8,128)(2,1)S(1)}, bf16[256,256]{1,0:T(8,128)(2,1)S(1)}, bf16[256,256]{1,0:T(8,128)(2,1)S(1)}, bf16[256,256]{1,0:T(8,128)(2,1)S(1)}) custom-call(bf16[256,256]{1,0:T(8,128)(2,1)} %q_hbm.1, bf16[256,256]{1,0:T(8,128)(2,1)} %k_hbm.1, bf16[256,256]{1,0:T(8,128)(2,1)} %v_hbm.1, bf16[256,1024]{1,0:T(8,128)(2,1)} %w_hbm.1, ...), custom_call_target="tpu_custom_call" | custom-call | tf_op jit(solution)/shard_map/pallas_call | solution.py:517
  25.9 0.8 %shard_map.85 = (bf16[64,1024]{1,0:T(8,128)(2,1)}, bf16[256,256]{1,0:T(8,128)(2,1)}, bf16[256,256]{1,0:T(8,128)(2,1)}, bf16[256,256]{1,0:T(8,128)(2,1)}) custom-call(bf16[64,1024]{1,0:T(8,128)(2,1)S(1)} %get-tuple-element.8.a0, bf16[256,256]{1,0:T(8,128)(2,1)S(1)} %get-tuple-element.9.a1, bf16[256,256]{1,0:T(8,128)(2,1)S(1)} %get-tuple-element.10.a2, ...), custom_call_target="tpu_custom_call" | custom-call | tf_op jit(solution)/shard_map/pallas_call | solution.py:560

commit v4 on v3

--- a/solution.py
+++ b/solution.py
@@ -263,16 +263,16 @@
     pl.semaphore_wait(barrier, n_seq - 1 + n_head - 1)
 
     for p in range(pairs):
+        @pl.when(me < n_seq - 1)
+        def _():
+            halo(p, 0).start()
+
+        @pl.when(me > 0)
+        def _():
+            halo(p, 1).start()
+
         for m in reversed(range(1, n_seq)):
             panel(p, m).start()
-
-        @pl.when(me < n_seq - 1)
-        def _():
-            halo(p, 0).start()
-
-        @pl.when(me > 0)
-        def _():
-            halo(p, 1).start()
 
     for load in loads[2 * pairs :]:
         load.wait()
@@ -375,8 +375,6 @@
         k_coarse = v_coarse = None
         for n in range(blocks):
             u = p * blocks + n
-            rows, cols = pl.ds(n * BLOCK, BLOCK), pl.ds(p * PAIR, PAIR)
-            kf, kc = keys(p, n, k_cols)
             vf, vc = keys(p, n, v_cols)
             qs, gs = qstack[u], gstack[u]
             pf = weights[u, pl.ds(0, window), :]
@@ -386,8 +384,8 @@
             dc = (pc.astype(F32) * (dot_nt(vc, gs) - dl)).astype(BF16)
             dvf, dvc = dot_nn(pf, gs), dot_nn(pc, gs)
             dkf, dkc = dot_nn(df, qs), dot_nn(dc, qs)
-            dq = heads_of(dot_tn(kf, df) + dot_tn(kc, dc)) * scale
-            qg_ref[rows, cols] = dq.T.astype(BF16)
+            weights[u, pl.ds(0, window), :] = df
+            weights[u, pl.ds(window, plan.coarse_rows), :] = dc
             for i in range(3):
                 piece = slice(i * BLOCK, (i + 1) * BLOCK)
                 old = k_parts[n + i]
@@ -421,6 +419,16 @@
         def _():
             rim(p, 1).start()
 
+    def query_part(p):
+        for n in range(blocks):
+            u = p * blocks + n
+            rows, cols = pl.ds(n * BLOCK, BLOCK), pl.ds(p * PAIR, PAIR)
+            kf, kc = keys(p, n, k_cols)
+            df = weights[u, pl.ds(0, window), :]
+            dc = weights[u, pl.ds(window, plan.coarse_rows), :]
+            dq = heads_of(dot_tn(kf, df) + dot_tn(kc, dc)) * scale
+            qg_ref[rows, cols] = dq.T.astype(BF16)
+
     share = frames // n_head
 
     def mix(m):
@@ -444,6 +452,7 @@
             for m in range(1, n_head):
                 mix(m).start()
         backward(p)
+        query_part(p)
 
     root = 1.0 / math.sqrt(plan.span)
     head_rows, tail_rows = pl.ds(0, BLOCK), pl.ds(frames - BLOCK, BLOCK)

time: 26.8 us -> 26.2 us (0.978)
  Pallas kernels: 26 us -> 25.4 us
    pallas_call x1, Pallas kernels: 25.2 us -> 24.6 us  [body(): pl.pallas_call(functools.partial(kernel, n_seq, n_head, plan), out_shape=...]
where the time goes in v4:
time: 26.2 us; the launch traced here: 26.1 us
  Pallas kernels  25.4 us (97%)
  between operations  0.64 us (2%)
    pallas_call x1, Pallas kernels, body(): pl.pallas_call(functools.partial(kernel, n_seq, n_head, plan), out_shape=...  24.6 us
    pallas_call x1, Pallas kernels, body(): pl.pallas_call(put_out, out_shape=shapes, in_specs=[pl.BlockSpec(memory_s...  0.82 us

profile of v4, /device:TPU:3, one launch (start us, length us, event | category | flops | bytes accessed | tf_op | source)
XLA Modules:
  0.0 26.1 jit_solution(2522503193658081406)
XLA Ops:
  0.6 24.6 %shard_map.84 = (bf16[64,1024]{1,0:T(8,128)(2,1)S(1)}, bf16[256,256]{1,0:T(8,128)(2,1)S(1)}, bf16[256,256]{1,0:T(8,128)(2,1)S(1)}, bf16[256,256]{1,0:T(8,128)(2,1)S(1)}) custom-call(bf16[256,256]{1,0:T(8,128)(2,1)} %q_hbm.1, bf16[256,256]{1,0:T(8,128)(2,1)} %k_hbm.1, bf16[256,256]{1,0:T(8,128)(2,1)} %v_hbm.1, bf16[256,1024]{1,0:T(8,128)(2,1)} %w_hbm.1, ...), custom_call_target="tpu_custom_call" | custom-call | tf_op jit(solution)/shard_map/pallas_call | solution.py:526
  25.2 0.8 %shard_map.85 = (bf16[64,1024]{1,0:T(8,128)(2,1)}, bf16[256,256]{1,0:T(8,128)(2,1)}, bf16[256,256]{1,0:T(8,128)(2,1)}, bf16[256,256]{1,0:T(8,128)(2,1)}) custom-call(bf16[64,1024]{1,0:T(8,128)(2,1)S(1)} %get-tuple-element.8.a0, bf16[256,256]{1,0:T(8,128)(2,1)S(1)} %get-tuple-element.9.a1, bf16[256,256]{1,0:T(8,128)(2,1)S(1)} %get-tuple-element.10.a2, ...), custom_call_target="tpu_custom_call" | custom-call | tf_op jit(solution)/shard_map/pallas_call | solution.py:569
